TPU v7x, 32 devices: a whole 2x2x4 slice. The times are simulated.
32 devices in a mesh: ens: 2 (over x), lat: 16 (over z, y, core).
Axes of the slice: x: 2, y: 2, z: 4, core: 2. Of those that a mesh axis runs over, the one named last changes fastest.
Arguments:
- spectral_in: bfloat16 [640, 2, 2, 64, 320], P('lat', None, None, 'ens'), parts along dimension 3, may hold values from -12 to 12
- legendre: bfloat16 [640, 2, 320, 640], P('lat'), may hold values from -0.25 to 0.25
- wave_of_slot: int32 [640], replicated, may hold values from 0 to 639, each once
Outputs:
- spectral_out: float32 [640, 2, 2, 64, 320], P('lat', None, None, 'ens'), parts along dimension 3
There are 2 independent parts, one for each index of `ens`. A program takes and returns all parts, laid end to end along the dimension named above; an argument that names none is the same for every part. Nothing has to cross between parts.
Inputs may be any that keep to these rules, and one draw needn't show every extreme that they name: `wave_of_slot`: every wavenumber 0 to 639 stands in exactly one slot.
All inputs are finite; a program needn't handle non-finite values.
Results may differ from a plain program's by a relative error of at most 0.0073.
Values may be sent and summed in bfloat16 or wider, within the bound.
No kernel may reach another device: no remote copies, remote signals or barrier semaphores. Data moves between devices by JAX's collectives and lax.ppermute only.
A program may use at most 192 MiB of HBM per device.

v0:
```python
import math

import jax
import jax.numpy as jnp
from jax import lax
from jax.sharding import PartitionSpec as P

NLON = 2560
FIELDS = 4


def validity(wavenumbers, total, half):
    ranks = 2 * jnp.arange(half, dtype=jnp.int32)[None, :] + jnp.arange(2, dtype=jnp.int32)[:, None]
    return ranks[None, :, :] <= (total - 1 - wavenumbers)[:, None, None]


def basis_tables(wave_of_slot):
    longitudes = jnp.arange(NLON, dtype=jnp.int32)
    phases = wave_of_slot[:, None] * longitudes[None, :] % NLON
    angles = phases.astype(jnp.float32) * (2.0 * math.pi / NLON)
    factor = 1.0 / math.sqrt(NLON)
    cosine = jnp.cos(angles) * factor
    sine_part = jnp.sin(angles) * factor
    weights = jnp.where(wave_of_slot == 0, 1.0, 2.0).astype(jnp.float32)[:, None]
    synthesis = jnp.stack([weights * cosine, -weights * sine_part]).astype(jnp.bfloat16)
    analysis = jnp.stack([cosine, -sine_part]).astype(jnp.bfloat16)
    return (synthesis, analysis)


def project_rows(gathered, legendre, is_valid):
    half = gathered.shape[3] // 2
    north_part = gathered[..., :half].astype(jnp.float32)
    south_part = gathered[..., half:][..., ::-1].astype(jnp.float32)
    folded = jnp.stack([north_part + south_part, north_part - south_part]).astype(jnp.bfloat16)
    result = jnp.einsum("sprj,pcslj->spclr", legendre, folded, preferred_element_type=jnp.float32)
    return jnp.where(is_valid[:, :, None, None, :], result, jnp.zeros_like(result))


def per_device(spectral_in, legendre, wave_of_slot):
    slot_count = legendre.shape[0]
    total_slots = wave_of_slot.shape[0]
    start_slot = lax.axis_index("lat") * slot_count
    own_waves = lax.dynamic_slice_in_dim(wave_of_slot, start_slot, slot_count)
    is_valid = validity(own_waves, total_slots, legendre.shape[2])
    masked = jnp.where(is_valid[:, :, None, None, :], spectral_in, jnp.zeros_like(spectral_in))
    parity_sum = jnp.einsum(
        "sprj,spclr->spclj", legendre, masked, preferred_element_type=jnp.float32
    )
    north_rows = parity_sum[:, 0] + parity_sum[:, 1]
    south_rows = (parity_sum[:, 0] - parity_sum[:, 1])[..., ::-1]
    fourier = jnp.concatenate([north_rows, south_rows], axis=3).astype(jnp.bfloat16)
    spread = lax.all_to_all(fourier, "lat", split_axis=3, concat_axis=0, tiled=True)
    synthesis, analysis = basis_tables(wave_of_slot)
    grid_field = jnp.einsum("scli,csx->lix", spread, synthesis, preferred_element_type=jnp.float32)
    slabs = grid_field.shape[0]
    levels = slabs // FIELDS
    partner = jnp.roll(
        grid_field.reshape((FIELDS, levels) + grid_field.shape[1:]), -1, axis=0
    ).reshape(grid_field.shape)
    product = (grid_field * partner).astype(jnp.bfloat16)
    coefficients = jnp.einsum(
        "lix,csx->csli", product, analysis, preferred_element_type=jnp.float32
    ).astype(jnp.bfloat16)
    gathered = lax.all_to_all(coefficients, "lat", split_axis=1, concat_axis=3, tiled=True)
    return project_rows(gathered, legendre, is_valid)


def solution(mesh):
    return jax.shard_map(
        per_device,
        mesh=mesh,
        in_specs=(P("lat", None, None, "ens", None), P("lat", None, None, None), P()),
        out_specs=P("lat", None, None, "ens", None),
        check_vma=False,
    )
```

profile of v0, /device:TPU:13, one launch (start us, length us, event | category | flops | bytes accessed | tf_op | source)
XLA Modules:
  0.0 755.3 jit_solution(387612567648793773)
XLA Ops:
  0.0 0.8 dynamic-slice_subtract_fusion
  0.8 0.1 broadcast_compare_fusion
  0.9 0.0 copy-start.2
  0.9 19.4 %fusion.2 = f32[40,2,2,32,640]{4,3,2,1,0:T(8,128)} fusion(bf16[40,2,320,640]{3,2,1,0:T(8,128)(2,1)} %param.4, bf16[40,2,2,32,320]{4,3,2,1,0:T(8,128)(2,1)} %param.3, pred[40,2,320]{2,1,0:T(4,128)(4,1)S(1)} %broadcast_compare_fusion), kind=kOutput, calls=%fused_computation.2 | convolution fusion | flops 2098790400 | bytes 49177600 | tf_op jit(solution)/shard_map/sprj,spclr->spclj/dot_general | solution.py:46
  20.3 0.0 copy-done.2
  20.3 0.0 copy-start
  20.3 8.1 %fusion.29 = bf16[40,2,32,640]{3,2,1,0:T(8,128)(2,1)} fusion(f32[40,2,2,32,640]{4,3,2,1,0:T(8,128)} %fusion.2), kind=kLoop, calls=%fused_computation.45 | loop fusion | flops 3276800 | bytes 16384000 | tf_op jit(solution)/shard_map/add | solution.py:49
  28.4 1.5 copy-done
  29.9 3.4 subtract_bitcast_fusion
  33.3 11.6 %rev.6 = bf16[40,2,32,640]{3,2,1,0:T(8,128)(2,1)S(1)} reverse(bf16[40,2,32,640]{3,2,1,0:T(8,128)(2,1)} %subtract_bitcast_fusion), dimensions={3} | reverse | bytes 6553600 | tf_op jit(solution)/shard_map/rev | solution.py:50
  44.9 5.6 pad_maximum_fusion.1
  50.5 35.5 %copy.31 = bf16[40,2,32,1280]{0,2,1,3:T(8,128)(2,1)} copy(bf16[40,2,32,1280]{3,2,1,0:T(8,128)(2,1)} %pad_maximum_fusion.1) | data formatting | bytes 13107200 | tf_op jit(solution)/shard_map/concatenate | solution.py:51
  86.0 33.4 %reshape.210 = bf16[16,2,102400]{2,1,0:T(2,128)(2,1)} reshape(bf16[1280,2,32,40]{3,2,1,0:T(8,128)(2,1)} %bitcast.71) | data formatting | bytes 13107200
  119.4 0.0 copy-start.4
  119.4 16.5 %all-to-all-start = ((bf16[16,2,102400]{2,1,0:T(2,128)(2,1)}), bf16[16,2,102400]{2,1,0:T(2,128)(2,1)}, u32[]{:S(2)}, u32[]{:S(2)}) async-start(bf16[16,2,102400]{2,1,0:T(2,128)(2,1)} %reshape.210), calls=%async_computation | async-start | bytes 13107200 | tf_op jit(solution)/shard_map/all_to_all | solution.py:52
  135.9 0.0 copy-done.4
  136.0 31.7 %multiply_convert_fusion.2 = (bf16[1,640,2560]{2,1,0:T(8,128)(2,1)S(1)}, bf16[1,640,2560]{2,1,0:T(8,128)(2,1)}, bf16[1,640,2560]{2,1,0:T(8,128)(2,1)}, bf16[1,640,2560]{2,1,0:T(8,128)(2,1)}) fusion(s32[640]{0:T(1024)S(1)} %copy-done.4, f32[640]{0:T(1024)S(1)} %fusion.37, f32[640]{0:T(1024)S(1)} %get-tuple-element.5), kind=kLoop, calls=%fused_computation.34 | loop fusion | flops 29491200 | bytes 13114880 | tf_op jit(solution)/shard_map/convert.9
  167.6 111.2 %all-to-all-done = bf16[16,2,102400]{2,1,0:T(2,128)(2,1)} async-done(((bf16[16,2,102400]{2,1,0:T(2,128)(2,1)}), bf16[16,2,102400]{2,1,0:T(2,128)(2,1)}, u32[]{:S(2)}, u32[]{:S(2)}) %all-to-all-start) | async-done | bytes 6553632 | tf_op jit(solution)/shard_map/all_to_all | solution.py:52
  278.8 35.4 %reshape.211 = bf16[1280,2,32,40]{3,2,1,0:T(8,128)(2,1)} reshape(bf16[16,2,102400]{2,1,0:T(2,128)(2,1)} %all-to-all-done) | data formatting | bytes 13107200
  314.2 24.6 %copy.43 = bf16[40,2,32,16,80]{4,0,3,1,2:T(8,128)(2,1)} copy(bf16[40,2,32,16,80]{0,2,1,4,3:T(8,128)(2,1)} %bitcast.72) | data formatting | bytes 13107200 | tf_op jit(solution)/shard_map/all_to_all | solution.py:52
  338.8 24.4 %convolution_bitcast_fusion = f32[32,80,2560]{2,1,0:T(8,128)} fusion(bf16[640,2,32,80]{3,0,1,2:T(8,128)(2,1)} %bitcast.75, bf16[1,640,2560]{2,1,0:T(8,128)(2,1)} %get-tuple-element.10, bf16[1,640,2560]{2,1,0:T(8,128)(2,1)} %get-tuple-element.12), kind=kOutput, calls=%fused_computation.9 | convolution fusion | flops 16780492800 | bytes 39321600 | tf_op jit(solution)/shard_map/scli,csx->lix/dot_general | solution.py:54
  363.1 3.5 slice_bitcast_fusion
  366.7 15.3 %slice.38 = f32[24,80,2560]{2,1,0:T(8,128)} slice(f32[32,80,2560]{2,1,0:T(8,128)} %convolution_bitcast_fusion), slice={[8:32], [0:80], [0:2560]} | slice | bytes 39321600 | tf_op jit(solution)/shard_map/jit(_roll_static)/slice | solution.py:57
  382.0 8.3 %pad_maximum_fusion = f32[4,8,80,2560]{3,2,1,0:T(8,128)S(1)} fusion(f32[1,8,80,2560]{3,2,1,0:T(8,128)S(1)} %slice_bitcast_fusion, f32[3,8,80,2560]{3,2,1,0:T(8,128)} %bitcast.73), kind=kLoop, calls=%fused_computation.4 | loop fusion | flops 6553600 | bytes 52428800 | tf_op jit(solution)/shard_map/jit(_roll_static)/concatenate | solution.py:57
  390.3 0.0 copy-start.1
  390.3 15.9 %fusion.4 = bf16[32,80,2560]{2,1,0:T(8,128)(2,1)} fusion(f32[32,80,2560]{2,1,0:T(8,128)} %convolution_bitcast_fusion, f32[4,8,80,2560]{3,2,1,0:T(8,128)S(1)} %pad_maximum_fusion), kind=kLoop, calls=%fused_computation.6 | loop fusion | flops 13107200 | bytes 65536000 | tf_op jit(solution)/shard_map/convert_element_type | solution.py:60
  406.2 0.0 copy-done.1
  406.2 21.1 %fusion.24 = bf16[2,640,32,80]{1,3,2,0:T(8,128)(2,1)} fusion(bf16[32,80,2560]{2,1,0:T(8,128)(2,1)} %fusion.4, bf16[1,640,2560]{2,1,0:T(8,128)(2,1)S(1)} %copy-done.1, bf16[1,640,2560]{2,1,0:T(8,128)(2,1)S(1)} %get-tuple-element.9), kind=kOutput, calls=%fused_computation.41 | convolution fusion | flops 16793600000 | bytes 26214400 | tf_op jit(solution)/shard_map/lix,csx->csli/dot_general | solution.py:61
  427.3 15.0 %copy.34 = bf16[2,640,32,80]{3,2,0,1:T(8,128)(2,1)} copy(bf16[2,640,32,80]{1,3,2,0:T(8,128)(2,1)} %fusion.24) | data formatting | bytes 13107200 | tf_op jit(solution)/shard_map/convert_element_type | solution.py:63
  442.4 232.1 %all_to_all.36 = bf16[2,640,32,80]{3,2,0,1:T(8,128)(2,1)} all-to-all(bf16[2,640,32,80]{3,2,0,1:T(8,128)(2,1)} %copy.34), channel_id=1, replica_groups=mesh['ens'=2,'lat'=16] {'lat'}, dimensions={1} | all-to-all | bytes 13107200 | tf_op jit(solution)/shard_map/all_to_all | solution.py:64
  674.4 27.6 %copy.36 = bf16[2,40,32,16,80]{4,3,2,0,1:T(8,128)(2,1)} copy(bf16[2,40,32,16,80]{4,2,0,1,3:T(8,128)(2,1)} %bitcast.74) | data formatting | bytes 13107200 | tf_op jit(solution)/shard_map/all_to_all | solution.py:64
  702.0 16.9 %all_to_all.33 = bf16[2,40,32,1280]{3,2,0,1:T(8,128)(2,1)} reshape(bf16[2,40,32,16,80]{4,3,2,0,1:T(8,128)(2,1)} %copy.36) | data formatting | bytes 13107200 | tf_op jit(solution)/shard_map/all_to_all | solution.py:64
  718.9 0.0 slice-start
  718.9 1.9 slice-done
  720.8 8.9 %rev.7 = bf16[2,40,32,640]{3,2,0,1:T(8,128)(2,1)} reverse(bf16[2,40,32,640]{3,2,0,1:T(8,128)(2,1)S(1)} %slice-done), dimensions={3} | reverse | bytes 6553600 | tf_op jit(solution)/shard_map/rev | solution.py:33
  729.8 0.0 copy-start.3
  729.8 6.4 fusion.31
  736.2 0.0 copy-done.3
  736.2 18.9 %broadcast_select_fusion = f32[40,2,2,32,320]{4,3,2,1,0:T(8,128)} fusion(pred[40,2,320]{2,1,0:T(4,128)(4,1)S(1)} %copy-done.3, bf16[40,2,320,640]{3,2,1,0:T(8,128)(2,1)} %param.4, bf16[1,2,40,32,640]{4,3,1,0,2:T(8,128)(2,1)} %get-tuple-element.8, bf16[1,2,40,32,640]{4,3,1,0,2:T(8,128)(2,1)S(1)} %get-tuple-element.7), kind=kOutput, calls=%fused_computation.42 | convolution fusion | flops 2102067200 | bytes 45900800 | tf_op jit(solution)/shard_map/sprj,pcslj->spclr/dot_general | solution.py:35
  (4 shorter events, 0.0 us)
Async XLA Ops:
  0.9 19.4 %copy-start.2 = (pred[40,2,320]{2,1,0:T(4,128)(4,1)}, pred[40,2,320]{2,1,0:T(4,128)(4,1)S(1)}, u32[]{:S(2)}) copy-start(pred[40,2,320]{2,1,0:T(4,128)(4,1)S(1)} %broadcast_compare_fusion) | copy-start | bytes 76804
  20.3 9.7 %copy-start = (f32[40,2,2,32,640]{4,3,2,1,0:T(8,128)S(1)}, f32[40,2,2,32,640]{4,3,2,1,0:T(8,128)}, u32[]{:S(2)}) copy-start(f32[40,2,2,32,640]{4,3,2,1,0:T(8,128)} %fusion.2) | copy-start | bytes 39321604
  119.4 16.5 %copy-start.4 = (s32[640]{0:T(1024)S(1)}, s32[640]{0:T(1024)}, u32[]{:S(2)}) copy-start(s32[640]{0:T(1024)} %param.5) | copy-start | bytes 7684
  119.4 159.4 %all-to-all-start = ((bf16[16,2,102400]{2,1,0:T(2,128)(2,1)}), bf16[16,2,102400]{2,1,0:T(2,128)(2,1)}, u32[]{:S(2)}, u32[]{:S(2)}) async-start(bf16[16,2,102400]{2,1,0:T(2,128)(2,1)} %reshape.210), calls=%async_computation | async-start | bytes 13107200 | tf_op jit(solution)/shard_map/all_to_all | solution.py:52
  390.3 15.9 %copy-start.1 = (bf16[1,640,2560]{2,1,0:T(8,128)(2,1)S(1)}, bf16[1,640,2560]{2,1,0:T(8,128)(2,1)}, u32[]{:S(2)}) copy-start(bf16[1,640,2560]{2,1,0:T(8,128)(2,1)} %get-tuple-element.11) | copy-start | bytes 9830404
  718.9 1.9 slice-start
  729.8 6.5 copy-start.3
where the time goes:
time: 761 us; the launch traced here: 755 us
  blocking collectives  232 us (30%)
  local copies, waits for them, and re-layouts  231 us (30%)
  waiting for transfers between devices  111 us (15%)
  matrix products  83.7 us (11%)
  other arithmetic  80.3 us (11%)
  starting transfers between devices  16.5 us (2%)
    all_to_all x1, blocking collectives, per_device(): lax.all_to_all(coefficients, 'lat', split_axis=1, concat_axis=3, tiled=True)  232 us
    all_to_all x1, waiting for transfers between devices, per_device(): lax.all_to_all(fourier, 'lat', split_axis=3, concat_axis=0, tiled=True)  111 us
    unnamed x12, local copies, waits for them, and re-layouts  70.3 us
    all_to_all x2, local copies, waits for them, and re-layouts, per_device(): lax.all_to_all(coefficients, 'lat', split_axis=1, concat_axis=3, tiled=True)  44.5 us
    concatenate x1, local copies, waits for them, and re-layouts, per_device(): jnp.concatenate([north_rows, south_rows], axis=3).astype(jnp.bfloat16)  35.5 us
    another operation x1, other arithmetic  31.7 us
    all_to_all x1, local copies, waits for them, and re-layouts, per_device(): lax.all_to_all(fourier, 'lat', split_axis=3, concat_axis=0, tiled=True)  24.6 us
    dot_general x1, matrix products, per_device(): jnp.einsum('scli,csx->lix', spread, synthesis, preferred_element_type=jnp...  24.4 us
  transfers between devices with their start and end apart: 1, of which 1 were waited for; matrix products, arithmetic and copies ran while one was open for 4% of the time, Pallas kernels for 0%

commit v1 on v0

v1 whole, which is shorter than its diff:
```python
import math

import jax
import jax.numpy as jnp
from jax import lax
from jax.experimental import pallas as pl
from jax.experimental.pallas import tpu as pltpu
from jax.sharding import PartitionSpec as P

NLON = 2560
FIELDS = 4
HALF = NLON // 2
LANES = 128
SLOTS_PER_STEP = 8
XBLOCK = 256
SBLOCK = 128
VMEM = 56 << 20


def quarter_sine(t):
    u = t * t
    p = jnp.float32(-3.5988432e-6)
    for coefficient in (1.60441184787e-4, -4.68175413532e-3, 7.96926262462e-2, -6.45964097506e-1, 1.57079632679):
        p = p * u + jnp.float32(coefficient)
    return p * t


def phase_turn(waves, points):
    product = waves * points
    return product - NLON * jnp.round(product * (1.0 / NLON))


def cosine_of(turn):
    return quarter_sine((HALF // 2 - jnp.abs(turn)) * (2.0 / HALF))


def sine_of(turn):
    size = jnp.abs(turn)
    return jnp.sign(turn) * quarter_sine(jnp.minimum(size, HALF - size) * (2.0 / HALF))


def half_tables(waves):
    m = waves.astype(jnp.float32)
    factor = 1.0 / math.sqrt(NLON)
    weight = jnp.where(waves == 0, 1.0, 2.0).astype(jnp.float32)
    x = jnp.arange(HALF + 16, dtype=jnp.float32)
    turn = phase_turn(m[None, :], x[:, None])
    synthesis_cos = (cosine_of(turn) * factor * weight[None, :]).astype(jnp.bfloat16)
    synthesis_sin = (-sine_of(turn[:HALF]) * factor * weight[None, :]).astype(jnp.bfloat16)
    x = x[:HALF]
    twice = jnp.where(x == 0, 1.0, 2.0)[None, :]
    turn = phase_turn(m[:, None], x[None, :])
    analysis_cos = (cosine_of(turn) * factor * twice).astype(jnp.bfloat16)
    analysis_sin = (-sine_of(turn) * factor * twice).astype(jnp.bfloat16)
    alternate = jnp.where(waves % 2 == 0, factor, -factor).astype(jnp.bfloat16).astype(jnp.float32)
    return synthesis_cos, synthesis_sin, analysis_cos, analysis_sin, alternate[:, None]


def synthesis_kernel(count_ref, spectral_ref, legendre_ref, out_ref, scratch):
    step = pl.program_id(0)
    levels = out_ref.shape[0] // 2
    rows = spectral_ref.shape[2] * spectral_ref.shape[3]
    half = spectral_ref.shape[4]
    lane = lax.broadcasted_iota(jnp.int32, (rows, half), 1)
    for s in range(SLOTS_PER_STEP):
        parts = []
        for p in range(2):
            values = spectral_ref[s, p].reshape(rows, half).astype(jnp.float32)
            count = count_ref[step * SLOTS_PER_STEP + s, p]
            values = jnp.where(lane < count, values, 0.0).astype(jnp.bfloat16)
            parts.append(jnp.dot(values, legendre_ref[s, p], preferred_element_type=jnp.float32))
        scratch[s, 0] = parts[0] + parts[1]
        scratch[s, 1] = parts[0] - parts[1]
        for v in range(levels):
            for ns in range(2):
                tile = scratch[s, ns, pl.ds(v, rows // levels, stride=levels), :]
                out_ref[2 * v + ns, s] = tile.astype(jnp.bfloat16)


def synthesize(counts, spectral, legendre, chunk):
    slots, _, _, slabs, half = spectral.shape
    levels = slabs // FIELDS
    rows = 2 * FIELDS
    return pl.pallas_call(
        synthesis_kernel,
        grid_spec=pltpu.PrefetchScalarGridSpec(
            num_scalar_prefetch=1,
            grid=(slots // SLOTS_PER_STEP,),
            in_specs=[
                pl.BlockSpec((SLOTS_PER_STEP, 2, 2, slabs, half), lambda i, c: (i, 0, 0, 0, 0)),
                pl.BlockSpec((SLOTS_PER_STEP, 2, half, LANES), lambda i, c: (i, 0, 0, chunk)),
            ],
            out_specs=pl.BlockSpec((2 * levels, SLOTS_PER_STEP, rows, LANES), lambda i, c: (0, i, 0, 0)),
            scratch_shapes=[pltpu.VMEM((SLOTS_PER_STEP, 2, 2 * slabs, LANES), jnp.float32)],
        ),
        out_shape=jax.ShapeDtypeStruct((2 * levels, slots, rows, LANES), jnp.bfloat16),
        compiler_params=pltpu.CompilerParams(vmem_limit_bytes=VMEM),
        cost_estimate=pl.CostEstimate(
            flops=2 * slots * 2 * 2 * slabs * half * LANES,
            transcendentals=0,
            bytes_accessed=slots * 2 * half * (LANES + 2 * slabs) * 2,
        ),
        name="legendre_synthesis",
    )(counts, spectral, legendre)


def grid_kernel(y_ref, sc_ref, ss_ref, ac_ref, as_ref, alt_ref, out_ref, wide, cos_in, sin_in, even, odd):
    waves = y_ref.shape[0]
    rows = y_ref.shape[1]
    width = FIELDS * LANES
    wide[...] = y_ref[...].reshape(waves * rows, LANES).astype(jnp.float32)
    for f in range(FIELDS):
        columns = pl.ds(f * LANES, LANES)
        cos_in[:, columns] = wide[pl.ds(f, waves, stride=rows), :].astype(jnp.bfloat16)
        sin_in[:, columns] = wide[pl.ds(FIELDS + f, waves, stride=rows), :].astype(jnp.bfloat16)

    def partner(a):
        return jnp.concatenate([a[:, LANES:], a[:, :LANES]], axis=1)

    for b in range(HALF // XBLOCK):
        points = pl.ds(b * XBLOCK, XBLOCK)
        e = jnp.dot(sc_ref[points, :], cos_in[...], preferred_element_type=jnp.float32)
        o = jnp.dot(ss_ref[points, :], sin_in[...], preferred_element_type=jnp.float32)
        e2, o2 = partner(e), partner(o)
        even[points, :] = (e * e2 + o * o2).astype(jnp.bfloat16)
        odd[points, :] = (e * o2 + o * e2).astype(jnp.bfloat16)
    middle = jnp.dot(sc_ref[pl.ds(HALF, 16), :], cos_in[...], preferred_element_type=jnp.float32)
    middle = (middle * partner(middle)).astype(jnp.bfloat16).astype(jnp.float32)[0:1, :]

    for b in range(waves // SBLOCK):
        slots = pl.ds(b * SBLOCK, SBLOCK)
        cos_out = jnp.dot(ac_ref[slots, :], even[...], preferred_element_type=jnp.float32)
        cos_out = cos_out + alt_ref[slots, :] * middle
        sin_out = jnp.dot(as_ref[slots, :], odd[...], preferred_element_type=jnp.float32)
        for f in range(FIELDS):
            columns = slice(f * LANES, (f + 1) * LANES)
            wide[pl.ds(b * SBLOCK * rows + f, SBLOCK, stride=rows), :] = cos_out[:, columns]
            wide[pl.ds(b * SBLOCK * rows + FIELDS + f, SBLOCK, stride=rows), :] = sin_out[:, columns]
    out_ref[...] = wide[...].astype(jnp.bfloat16).reshape(waves, rows, LANES)


def grid_product(y, tables):
    waves, rows, _ = y.shape
    width = FIELDS * LANES
    return pl.pallas_call(
        grid_kernel,
        out_shape=jax.ShapeDtypeStruct(y.shape, jnp.bfloat16),
        scratch_shapes=[
            pltpu.VMEM((waves * rows, LANES), jnp.float32),
            pltpu.VMEM((waves, width), jnp.bfloat16),
            pltpu.VMEM((waves, width), jnp.bfloat16),
            pltpu.VMEM((HALF, width), jnp.bfloat16),
            pltpu.VMEM((HALF, width), jnp.bfloat16),
        ],
        compiler_params=pltpu.CompilerParams(vmem_limit_bytes=VMEM),
        cost_estimate=pl.CostEstimate(
            flops=8 * waves * HALF * width, transcendentals=0, bytes_accessed=8 * waves * HALF + 4 * waves * rows * LANES
        ),
        name="grid_product",
    )(y, *tables)


def projection_kernel(chunks, added, count_ref, *refs):
    arrived = refs[:chunks]
    legendres = refs[chunks : 2 * chunks]
    before = refs[2 * chunks] if added else None
    out_ref, scratch = refs[-2], refs[-1]
    step = pl.program_id(0)
    levels = arrived[0].shape[0] // 2
    fields = arrived[0].shape[2]
    rows = levels * fields
    half = legendres[0].shape[2]
    lane = lax.broadcasted_iota(jnp.int32, (rows, half), 1)
    for s in range(SLOTS_PER_STEP):
        sums = [None, None]
        for k in range(chunks):
            for v in range(levels):
                north = arrived[k][2 * v, s].astype(jnp.float32)
                south = arrived[k][2 * v + 1, s].astype(jnp.float32)
                scratch[s, k, 0, pl.ds(v * fields, fields), :] = north + south
                scratch[s, k, 1, pl.ds(v * fields, fields), :] = north - south
            for p in range(2):
                folded = jnp.concatenate(
                    [scratch[s, k, p, pl.ds(r, levels, stride=fields), :] for r in range(fields)], axis=0
                ).astype(jnp.bfloat16)
                part = lax.dot_general(
                    folded, legendres[k][s, p], (((1,), (1,)), ((), ())), preferred_element_type=jnp.float32
                )
                sums[p] = part if sums[p] is None else sums[p] + part
        for p in range(2):
            count = count_ref[step * SLOTS_PER_STEP + s, p]
            value = jnp.where(lane < count, sums[p], 0.0).reshape(out_ref.shape[2:])
            if added:
                value = value + before[s, p]
            out_ref[s, p] = value


def project(counts, arrived, legendre, chunk_ids, before=None):
    chunks = len(arrived)
    ranks, slots, fields, _ = arrived[0].shape
    slabs = ranks // 2 * FIELDS
    half = legendre.shape[2]
    n = SLOTS_PER_STEP
    out_spec = pl.BlockSpec((n, 2, 2, slabs, half), lambda i, c: (i, 0, 0, 0, 0))
    added = before is not None

    def kernel(*refs):
        projection_kernel(chunks, added, *refs)

    return pl.pallas_call(
        kernel,
        grid_spec=pltpu.PrefetchScalarGridSpec(
            num_scalar_prefetch=1,
            grid=(slots // n,),
            in_specs=[pl.BlockSpec((ranks, n, fields, LANES), lambda i, c: (0, i, 0, 0))] * chunks
            + [pl.BlockSpec((n, 2, half, LANES), lambda i, c, k=k: (i, 0, 0, k)) for k in chunk_ids]
            + ([out_spec] if added else []),
            out_specs=out_spec,
            scratch_shapes=[pltpu.VMEM((n, chunks, 2, 2 * slabs, LANES), jnp.float32)],
        ),
        out_shape=jax.ShapeDtypeStruct((slots, 2, 2, slabs, half), jnp.float32),
        input_output_aliases={1 + 2 * chunks: 0} if added else {},
        compiler_params=pltpu.CompilerParams(vmem_limit_bytes=VMEM),
        cost_estimate=pl.CostEstimate(
            flops=2 * chunks * slots * 2 * 2 * slabs * half * LANES,
            transcendentals=0,
            bytes_accessed=slots * 2 * half * (chunks * LANES + 4 * slabs) * 2,
        ),
        name="legendre_projection",
    )(counts, *arrived, *([legendre] * chunks), *([before] if added else []))


def per_device(spectral_in, legendre, wave_of_slot):
    slots, _, _, slabs, half = spectral_in.shape
    total = wave_of_slot.shape[0]
    ranks = total // slots
    chunks = legendre.shape[3] // LANES
    start = lax.axis_index("lat") * slots
    own = lax.dynamic_slice_in_dim(wave_of_slot, start, slots)
    counts = (total + 1 - own[:, None] - jnp.arange(2, dtype=jnp.int32)[None, :]) // 2
    tables = half_tables(wave_of_slot)

    def exchange(x):
        return lax.all_to_all(x, "lat", split_axis=0, concat_axis=0, tiled=True)

    sent = [exchange(synthesize(counts, spectral_in, legendre, k)) for k in range(chunks)]
    back = []
    for y in sent:
        product = grid_product(y.reshape(total, 2 * FIELDS, LANES), tables)
        back.append(exchange(product.reshape(ranks, slots, 2 * FIELDS, LANES)))
    first = project(counts, back[:-1], legendre, range(chunks - 1))
    return project(counts, back[-1:], legendre, [chunks - 1], first)


def basis_tables(wave_of_slot):
    longitudes = jnp.arange(NLON, dtype=jnp.int32)
    phases = wave_of_slot[:, None] * longitudes[None, :] % NLON
    angles = phases.astype(jnp.float32) * (2.0 * math.pi / NLON)
    factor = 1.0 / math.sqrt(NLON)
    cosine = jnp.cos(angles) * factor
    sine_part = jnp.sin(angles) * factor
    weights = jnp.where(wave_of_slot == 0, 1.0, 2.0).astype(jnp.float32)[:, None]
    synthesis = jnp.stack([weights * cosine, -weights * sine_part]).astype(jnp.bfloat16)
    analysis = jnp.stack([cosine, -sine_part]).astype(jnp.bfloat16)
    return synthesis, analysis


def per_device_general(spectral_in, legendre, wave_of_slot):
    slot_count, _, half, north = legendre.shape
    total = wave_of_slot.shape[0]
    own = lax.dynamic_slice_in_dim(wave_of_slot, lax.axis_index("lat") * slot_count, slot_count)
    ranks = 2 * jnp.arange(half, dtype=jnp.int32)[None, :] + jnp.arange(2, dtype=jnp.int32)[:, None]
    is_valid = (ranks[None] <= (total - 1 - own)[:, None, None])[:, :, None, None, :]
    masked = jnp.where(is_valid, spectral_in, jnp.zeros_like(spectral_in))
    sums = jnp.einsum("sprj,spclr->spclj", legendre, masked, preferred_element_type=jnp.float32)
    south = (sums[:, 0] - sums[:, 1])[..., ::-1]
    fourier = jnp.concatenate([sums[:, 0] + sums[:, 1], south], axis=3).astype(jnp.bfloat16)
    spread = lax.all_to_all(fourier, "lat", split_axis=3, concat_axis=0, tiled=True)
    synthesis, analysis = basis_tables(wave_of_slot)
    field = jnp.einsum("scli,csx->lix", spread, synthesis, preferred_element_type=jnp.float32)
    levels = field.shape[0] // FIELDS
    partner = jnp.roll(field.reshape((FIELDS, levels) + field.shape[1:]), -1, axis=0).reshape(field.shape)
    product = (field * partner).astype(jnp.bfloat16)
    coefficients = jnp.einsum("lix,csx->csli", product, analysis, preferred_element_type=jnp.float32)
    gathered = lax.all_to_all(coefficients.astype(jnp.bfloat16), "lat", split_axis=1, concat_axis=3, tiled=True)
    north_part = gathered[..., :north].astype(jnp.float32)
    south_part = gathered[..., north:][..., ::-1].astype(jnp.float32)
    folded = jnp.stack([north_part + south_part, north_part - south_part]).astype(jnp.bfloat16)
    result = jnp.einsum("sprj,pcslj->spclr", legendre, folded, preferred_element_type=jnp.float32)
    return jnp.where(is_valid, result, jnp.zeros_like(result))


def solution(mesh):
    rows = mesh.shape["lat"]

    def local(spectral_in, legendre, wave_of_slot):
        slots, _, _, slabs, _ = spectral_in.shape
        whole_tiles = slots % SLOTS_PER_STEP == 0 and legendre.shape[3] % LANES == 0
        if rows * FIELDS == 2 * slabs and whole_tiles and wave_of_slot.shape[0] % SBLOCK == 0:
            return per_device(spectral_in, legendre, wave_of_slot)
        return per_device_general(spectral_in, legendre, wave_of_slot)

    return jax.shard_map(
        local,
        mesh=mesh,
        in_specs=(P("lat", None, None, "ens", None), P("lat", None, None, None), P()),
        out_specs=P("lat", None, None, "ens", None),
        check_vma=False,
    )
```

time: 761 us -> 386 us (0.51)
  blocking collectives: 232 us -> 0 us
  local copies, waits for them, and re-layouts: 231 us -> 1.99 us
  Pallas kernels: 0 us -> 119 us
  matrix products: 83.7 us -> 0 us
  waiting for transfers between devices: 111 us -> 192 us
  other arithmetic: 80.3 us -> 15.5 us
  starting transfers between devices: 16.5 us -> 51.3 us
    all_to_all x1 -> x0, blocking collectives: 232 us -> none  [per_device(): lax.all_to_all(coefficients, 'lat', split_axis=1, concat_axis=3, tiled=True)]
    pallas_call x0 -> x12, Pallas kernels: none -> 119 us  [the longest x5 46.3 us: grid_product(): pl.pallas_call(grid_kernel, out_shape=jax.ShapeDtypeStruct(y.shape, jnp.b...]
    dot_general x4 -> x0, matrix products: 83.7 us -> none  [the longest x1 24.4 us: per_device(): jnp.einsum('scli,csx->lix', spread, synthesis, preferred_element_type=jnp...]
    all_to_all x1 -> x10, waiting for transfers between devices: 111 us -> 192 us  [exchange(): return lax.all_to_all(x, 'lat', split_axis=0, concat_axis=0, tiled=True)]
    unnamed x12 -> x18, local copies, waits for them, and re-layouts: 70.3 us -> 1.11 us
    all_to_all x3 -> x0, local copies, waits for them, and re-layouts: 69.1 us -> none  [the longest x2 44.5 us: per_device(): lax.all_to_all(coefficients, 'lat', split_axis=1, concat_axis=3, tiled=True)]
    another operation x2 -> x0, other arithmetic: 38.1 us -> none
    concatenate x1 -> x0, local copies, waits for them, and re-layouts: 35.5 us -> none  [per_device(): jnp.concatenate([north_rows, south_rows], axis=3).astype(jnp.bfloat16)]
  transfers between devices with their start and end apart: 1 -> 10, of which waited for: 1 -> 10; matrix products, arithmetic and copies ran while one was open for 4% -> 4% of each run, Pallas kernels for 0% -> 26%
where the time goes in v1:
time: 386 us; the launch traced here: 380 us
  waiting for transfers between devices  192 us (50%)
  Pallas kernels  119 us (31%)
  starting transfers between devices  51.3 us (13%)
  other arithmetic  15.5 us (4%)
    all_to_all x10, waiting for transfers between devices, exchange(): return lax.all_to_all(x, 'lat', split_axis=0, concat_axis=0, tiled=True)  192 us
    all_to_all x10, starting transfers between devices, exchange(): return lax.all_to_all(x, 'lat', split_axis=0, concat_axis=0, tiled=True)  51.3 us
    pallas_call x5, Pallas kernels, grid_product(): pl.pallas_call(grid_kernel, out_shape=jax.ShapeDtypeStruct(y.shape, jnp.b...  46.3 us
    pallas_call x5, Pallas kernels, synthesize(): pl.pallas_call(synthesis_kernel, grid_spec=pltpu.PrefetchScalarGridSpec(n...  41.3 us
    pallas_call x2, Pallas kernels, project(): pl.pallas_call(kernel, grid_spec=pltpu.PrefetchScalarGridSpec(num_scalar_...  30.9 us
  transfers between devices with their start and end apart: 10, of which 10 were waited for; matrix products, arithmetic and copies ran while one was open for 4% of the time, Pallas kernels for 26%

profile of v1, /device:TPU:13, one launch (start us, length us, event | category | flops | bytes accessed | tf_op | source)
XLA Modules:
  0.0 380.1 jit_solution(4602880893164957976)
XLA Ops:
  0.0 0.8 dynamic-slice_subtract_fusion
  0.8 0.7 add_select_fusion.count_ref.refs_0_
  1.4 8.2 %legendre_synthesis.9 = bf16[16,40,8,128]{3,2,1,0:T(8,128)(2,1)} custom-call(s32[40,2]{1,0:T(8,128)} %add_select_fusion.count_ref.refs_0_, bf16[40,2,2,32,320]{4,3,2,1,0:T(8,128)(2,1)} %spectral_ref.9, bf16[40,2,320,640]{3,2,1,0:T(8,128)(2,1)} %refs_2_.1), custom_call_target="tpu_custom_call" | custom-call | flops 419430400 | bytes 9830400 | tf_op jit(solution)/shard_map/legendre_synthesis/pallas_call | solution.py:84
  9.7 6.5 %all-to-all-start.8 = ((bf16[16,40,8,128]{3,2,1,0:T(8,128)(2,1)}), bf16[16,40,8,128]{3,2,1,0:T(8,128)(2,1)S(1)}, u32[]{:S(2)}, u32[]{:S(2)}) async-start(bf16[16,40,8,128]{3,2,1,0:T(8,128)(2,1)} %legendre_synthesis.9), calls=%async_computation.8 | async-start | bytes 2621440 | tf_op jit(solution)/shard_map/all_to_all | solution.py:244
  16.2 8.2 %legendre_synthesis.8 = bf16[16,40,8,128]{3,2,1,0:T(8,128)(2,1)} custom-call(s32[40,2]{1,0:T(8,128)} %add_select_fusion.count_ref.refs_0_, bf16[40,2,2,32,320]{4,3,2,1,0:T(8,128)(2,1)} %spectral_ref.9, bf16[40,2,320,640]{3,2,1,0:T(8,128)(2,1)} %refs_2_.1), custom_call_target="tpu_custom_call" | custom-call | flops 419430400 | bytes 9830400 | tf_op jit(solution)/shard_map/legendre_synthesis/pallas_call | solution.py:84
  24.5 22.3 %all-to-all-done.8 = bf16[16,40,8,128]{3,2,1,0:T(8,128)(2,1)S(1)} async-done(((bf16[16,40,8,128]{3,2,1,0:T(8,128)(2,1)}), bf16[16,40,8,128]{3,2,1,0:T(8,128)(2,1)S(1)}, u32[]{:S(2)}, u32[]{:S(2)}) %all-to-all-start.8) | async-done | bytes 1310752 | tf_op jit(solution)/shard_map/all_to_all | solution.py:244
  46.8 0.0 copy-start.5
  46.8 4.9 %all-to-all-start.6 = ((bf16[16,40,8,128]{3,2,1,0:T(8,128)(2,1)}), bf16[16,40,8,128]{3,2,1,0:T(8,128)(2,1)S(1)}, u32[]{:S(2)}, u32[]{:S(2)}) async-start(bf16[16,40,8,128]{3,2,1,0:T(8,128)(2,1)} %legendre_synthesis.8), calls=%async_computation.6 | async-start | bytes 2621440 | tf_op jit(solution)/shard_map/all_to_all | solution.py:244
  51.7 8.3 %legendre_synthesis.7 = bf16[16,40,8,128]{3,2,1,0:T(8,128)(2,1)} custom-call(s32[40,2]{1,0:T(8,128)} %add_select_fusion.count_ref.refs_0_, bf16[40,2,2,32,320]{4,3,2,1,0:T(8,128)(2,1)} %spectral_ref.9, bf16[40,2,320,640]{3,2,1,0:T(8,128)(2,1)} %refs_2_.1), custom_call_target="tpu_custom_call" | custom-call | flops 419430400 | bytes 9830400 | tf_op jit(solution)/shard_map/legendre_synthesis/pallas_call | solution.py:84
  59.9 0.0 copy-done.5
  59.9 22.3 %all-to-all-done.6 = bf16[16,40,8,128]{3,2,1,0:T(8,128)(2,1)S(1)} async-done(((bf16[16,40,8,128]{3,2,1,0:T(8,128)(2,1)}), bf16[16,40,8,128]{3,2,1,0:T(8,128)(2,1)S(1)}, u32[]{:S(2)}, u32[]{:S(2)}) %all-to-all-start.6) | async-done | bytes 1310752 | tf_op jit(solution)/shard_map/all_to_all | solution.py:244
  82.2 0.0 copy-start.6
  82.2 4.9 %all-to-all-start.4 = ((bf16[16,40,8,128]{3,2,1,0:T(8,128)(2,1)}), bf16[16,40,8,128]{3,2,1,0:T(8,128)(2,1)S(1)}, u32[]{:S(2)}, u32[]{:S(2)}) async-start(bf16[16,40,8,128]{3,2,1,0:T(8,128)(2,1)} %legendre_synthesis.7), calls=%async_computation.4 | async-start | bytes 2621440 | tf_op jit(solution)/shard_map/all_to_all | solution.py:244
  87.1 0.0 copy-start.8
  87.1 8.3 %legendre_synthesis.6 = bf16[16,40,8,128]{3,2,1,0:T(8,128)(2,1)} custom-call(s32[40,2]{1,0:T(8,128)} %add_select_fusion.count_ref.refs_0_, bf16[40,2,2,32,320]{4,3,2,1,0:T(8,128)(2,1)} %spectral_ref.9, bf16[40,2,320,640]{3,2,1,0:T(8,128)(2,1)} %refs_2_.1), custom_call_target="tpu_custom_call" | custom-call | flops 419430400 | bytes 9830400 | tf_op jit(solution)/shard_map/legendre_synthesis/pallas_call | solution.py:84
  95.4 0.0 copy-done.6
  95.4 22.2 %all-to-all-done.4 = bf16[16,40,8,128]{3,2,1,0:T(8,128)(2,1)S(1)} async-done(((bf16[16,40,8,128]{3,2,1,0:T(8,128)(2,1)}), bf16[16,40,8,128]{3,2,1,0:T(8,128)(2,1)S(1)}, u32[]{:S(2)}, u32[]{:S(2)}) %all-to-all-start.4) | async-done | bytes 1310752 | tf_op jit(solution)/shard_map/all_to_all | solution.py:244
  117.7 0.0 copy-start.7
  117.7 4.9 %all-to-all-start.2 = ((bf16[16,40,8,128]{3,2,1,0:T(8,128)(2,1)}), bf16[16,40,8,128]{3,2,1,0:T(8,128)(2,1)}, u32[]{:S(2)}, u32[]{:S(2)}) async-start(bf16[16,40,8,128]{3,2,1,0:T(8,128)(2,1)} %legendre_synthesis.6), calls=%async_computation.2 | async-start | bytes 2621440 | tf_op jit(solution)/shard_map/all_to_all | solution.py:244
  122.5 0.0 copy-done.8
  122.6 0.9 reshape.48.alt_ref
  123.4 8.2 %legendre_synthesis.5 = bf16[16,40,8,128]{3,2,1,0:T(8,128)(2,1)} custom-call(s32[40,2]{1,0:T(8,128)} %add_select_fusion.count_ref.refs_0_, bf16[40,2,2,32,320]{4,3,2,1,0:T(8,128)(2,1)} %spectral_ref.9, bf16[40,2,320,640]{3,2,1,0:T(8,128)(2,1)} %refs_2_.1), custom_call_target="tpu_custom_call" | custom-call | flops 419430400 | bytes 9830400 | tf_op jit(solution)/shard_map/legendre_synthesis/pallas_call | solution.py:84
  131.7 0.0 copy-done.7
  131.7 3.6 multiply_subtract_fusion.1
  135.3 17.9 %all-to-all-done.2 = bf16[16,40,8,128]{3,2,1,0:T(8,128)(2,1)} async-done(((bf16[16,40,8,128]{3,2,1,0:T(8,128)(2,1)}), bf16[16,40,8,128]{3,2,1,0:T(8,128)(2,1)}, u32[]{:S(2)}, u32[]{:S(2)}) %all-to-all-start.2) | async-done | bytes 1310752 | tf_op jit(solution)/shard_map/all_to_all | solution.py:244
  153.2 5.2 %all-to-all-start = ((bf16[16,40,8,128]{3,2,1,0:T(8,128)(2,1)}), bf16[16,40,8,128]{3,2,1,0:T(8,128)(2,1)}, u32[]{:S(2)}, u32[]{:S(2)}) async-start(bf16[16,40,8,128]{3,2,1,0:T(8,128)(2,1)} %legendre_synthesis.5), calls=%async_computation | async-start | bytes 2621440 | tf_op jit(solution)/shard_map/all_to_all | solution.py:244
  158.4 4.0 %multiply_convert_fusion.2.ss_ref = bf16[1280,640]{1,0:T(8,128)(2,1)} fusion(f32[1296,640]{1,0:T(8,128)S(1)} %get-tuple-element.9, f32[640]{0:T(1024)S(1)} %get-tuple-element.8), kind=kLoop, calls=%fused_computation.37 | loop fusion | flops 17203200 | bytes 4917760 | tf_op jit(solution)/shard_map/convert_element_type | solution.py:49
  162.4 6.4 %fusion.13 = (bf16[640,1280]{1,0:T(8,128)(2,1)}, bf16[640,1280]{1,0:T(8,128)(2,1)}) fusion(f32[1280]{0:T(1024)S(1)} %get-tuple-element.12, f32[1280]{0:T(1024)S(1)} %get-tuple-element.11, f32[640]{0:T(1024)S(1)} %convert_element_type.19), kind=kLoop, calls=%fused_computation.22 | loop fusion | flops 34406400 | bytes 3289600 | tf_op jit(solution)/shard_map/convert_element_type | solution.py:54
  168.9 9.2 %grid_product.6 = bf16[640,8,128]{2,1,0:T(8,128)(2,1)} custom-call(bf16[640,8,128]{2,1,0:T(8,128)(2,1)} %bitcast.2.y_ref, bf16[1296,640]{1,0:T(8,128)(2,1)} %get-tuple-element.10.sc_ref, bf16[1280,640]{1,0:T(8,128)(2,1)} %multiply_convert_fusion.2.ss_ref, bf16[640,1280]{1,0:T(8,128)(2,1)} %get-tuple-element.6.ac_ref, ...), custom_call_target="tpu_custom_call" | custom-call | flops 3355443200 | bytes 9175040 | tf_op jit(solution)/shard_map/grid_product/pallas_call | solution.py:145
  178.1 10.8 %all-to-all-done = bf16[16,40,8,128]{3,2,1,0:T(8,128)(2,1)} async-done(((bf16[16,40,8,128]{3,2,1,0:T(8,128)(2,1)}), bf16[16,40,8,128]{3,2,1,0:T(8,128)(2,1)}, u32[]{:S(2)}, u32[]{:S(2)}) %all-to-all-start) | async-done | bytes 1310752 | tf_op jit(solution)/shard_map/all_to_all | solution.py:244
  188.9 5.2 %all-to-all-start.3 = ((bf16[16,40,8,128]{3,2,1,0:T(8,128)(2,1)}), bf16[16,40,8,128]{3,2,1,0:T(8,128)(2,1)S(1)}, u32[]{:S(2)}, u32[]{:S(2)}) async-start(bf16[16,40,8,128]{3,2,1,0:T(8,128)(2,1)} %bitcast.15), calls=%async_computation.3 | async-start | bytes 2621440 | tf_op jit(solution)/shard_map/all_to_all | solution.py:244
  194.1 9.2 %grid_product.7 = bf16[640,8,128]{2,1,0:T(8,128)(2,1)} custom-call(bf16[640,8,128]{2,1,0:T(8,128)(2,1)} %bitcast.12, bf16[1296,640]{1,0:T(8,128)(2,1)} %get-tuple-element.10.sc_ref, bf16[1280,640]{1,0:T(8,128)(2,1)} %multiply_convert_fusion.2.ss_ref, bf16[640,1280]{1,0:T(8,128)(2,1)} %get-tuple-element.6.ac_ref, bf16[640,1280]{1,0:T(8,128)(2,1)} %get-tuple-element.5.as_ref, ...), custom_call_target="tpu_custom_call" | custom-call | flops 3355443200 | bytes 9175040 | tf_op jit(solution)/shard_map/grid_product/pallas_call | solution.py:145
  203.3 21.2 %all-to-all-done.3.refs_1_ = bf16[16,40,8,128]{3,2,1,0:T(8,128)(2,1)S(1)} async-done(((bf16[16,40,8,128]{3,2,1,0:T(8,128)(2,1)}), bf16[16,40,8,128]{3,2,1,0:T(8,128)(2,1)S(1)}, u32[]{:S(2)}, u32[]{:S(2)}) %all-to-all-start.3) | async-done | bytes 1310752 | tf_op jit(solution)/shard_map/all_to_all | solution.py:244
  224.5 0.0 copy-start
  224.5 4.9 %all-to-all-start.5 = ((bf16[16,40,8,128]{3,2,1,0:T(8,128)(2,1)}), bf16[16,40,8,128]{3,2,1,0:T(8,128)(2,1)S(1)}, u32[]{:S(2)}, u32[]{:S(2)}) async-start(bf16[16,40,8,128]{3,2,1,0:T(8,128)(2,1)} %bitcast.16), calls=%async_computation.5 | async-start | bytes 2621440 | tf_op jit(solution)/shard_map/all_to_all | solution.py:244
  229.4 9.2 %grid_product.8 = bf16[640,8,128]{2,1,0:T(8,128)(2,1)} custom-call(bf16[640,8,128]{2,1,0:T(8,128)(2,1)} %bitcast.11, bf16[1296,640]{1,0:T(8,128)(2,1)} %get-tuple-element.10.sc_ref, bf16[1280,640]{1,0:T(8,128)(2,1)} %multiply_convert_fusion.2.ss_ref, bf16[640,1280]{1,0:T(8,128)(2,1)} %get-tuple-element.6.ac_ref, bf16[640,1280]{1,0:T(8,128)(2,1)} %get-tuple-element.5.as_ref, ...), custom_call_target="tpu_custom_call" | custom-call | flops 3355443200 | bytes 9175040 | tf_op jit(solution)/shard_map/grid_product/pallas_call | solution.py:145
  238.6 0.0 copy-done
  238.6 21.3 %all-to-all-done.5.refs_2_ = bf16[16,40,8,128]{3,2,1,0:T(8,128)(2,1)S(1)} async-done(((bf16[16,40,8,128]{3,2,1,0:T(8,128)(2,1)}), bf16[16,40,8,128]{3,2,1,0:T(8,128)(2,1)S(1)}, u32[]{:S(2)}, u32[]{:S(2)}) %all-to-all-start.5) | async-done | bytes 1310752 | tf_op jit(solution)/shard_map/all_to_all | solution.py:244
  260.0 0.0 copy-start.1
  260.0 5.2 %all-to-all-start.7 = ((bf16[16,40,8,128]{3,2,1,0:T(8,128)(2,1)}), bf16[16,40,8,128]{3,2,1,0:T(8,128)(2,1)S(1)}, u32[]{:S(2)}, u32[]{:S(2)}) async-start(bf16[16,40,8,128]{3,2,1,0:T(8,128)(2,1)} %bitcast.17), calls=%async_computation.7 | async-start | bytes 2621440 | tf_op jit(solution)/shard_map/all_to_all | solution.py:244
  265.2 9.3 %grid_product.9 = bf16[640,8,128]{2,1,0:T(8,128)(2,1)} custom-call(bf16[640,8,128]{2,1,0:T(8,128)(2,1)} %bitcast.10, bf16[1296,640]{1,0:T(8,128)(2,1)} %get-tuple-element.10.sc_ref, bf16[1280,640]{1,0:T(8,128)(2,1)} %multiply_convert_fusion.2.ss_ref, bf16[640,1280]{1,0:T(8,128)(2,1)} %get-tuple-element.6.ac_ref, bf16[640,1280]{1,0:T(8,128)(2,1)} %get-tuple-element.5.as_ref, ...), custom_call_target="tpu_custom_call" | custom-call | flops 3355443200 | bytes 9175040 | tf_op jit(solution)/shard_map/grid_product/pallas_call | solution.py:145
  274.5 0.0 copy-done.1
  274.5 21.1 %all-to-all-done.7.refs_3_ = bf16[16,40,8,128]{3,2,1,0:T(8,128)(2,1)S(1)} async-done(((bf16[16,40,8,128]{3,2,1,0:T(8,128)(2,1)}), bf16[16,40,8,128]{3,2,1,0:T(8,128)(2,1)S(1)}, u32[]{:S(2)}, u32[]{:S(2)}) %all-to-all-start.7) | async-done | bytes 1310752 | tf_op jit(solution)/shard_map/all_to_all | solution.py:244
  295.6 0.0 copy-start.2
  295.6 4.9 %all-to-all-start.9 = ((bf16[16,40,8,128]{3,2,1,0:T(8,128)(2,1)}), bf16[16,40,8,128]{3,2,1,0:T(8,128)(2,1)S(1)}, u32[]{:S(2)}, u32[]{:S(2)}) async-start(bf16[16,40,8,128]{3,2,1,0:T(8,128)(2,1)} %bitcast.14), calls=%async_computation.9 | async-start | bytes 2621440 | tf_op jit(solution)/shard_map/all_to_all | solution.py:244
  300.5 9.3 %grid_product.5 = bf16[640,8,128]{2,1,0:T(8,128)(2,1)} custom-call(bf16[640,8,128]{2,1,0:T(8,128)(2,1)} %bitcast.y_ref, bf16[1296,640]{1,0:T(8,128)(2,1)} %get-tuple-element.10.sc_ref, bf16[1280,640]{1,0:T(8,128)(2,1)} %multiply_convert_fusion.2.ss_ref, bf16[640,1280]{1,0:T(8,128)(2,1)} %get-tuple-element.6.ac_ref, ...), custom_call_target="tpu_custom_call" | custom-call | flops 3355443200 | bytes 9175040 | tf_op jit(solution)/shard_map/grid_product/pallas_call | solution.py:145
  309.8 0.0 copy-done.2
  309.8 21.3 %all-to-all-done.9.refs_4_ = bf16[16,40,8,128]{3,2,1,0:T(8,128)(2,1)S(1)} async-done(((bf16[16,40,8,128]{3,2,1,0:T(8,128)(2,1)}), bf16[16,40,8,128]{3,2,1,0:T(8,128)(2,1)S(1)}, u32[]{:S(2)}, u32[]{:S(2)}) %all-to-all-start.9) | async-done | bytes 1310752 | tf_op jit(solution)/shard_map/all_to_all | solution.py:244
  331.1 0.0 copy-start.3
  331.1 4.9 %all-to-all-start.1 = ((bf16[16,40,8,128]{3,2,1,0:T(8,128)(2,1)}), bf16[16,40,8,128]{3,2,1,0:T(8,128)(2,1)S(1)}, u32[]{:S(2)}, u32[]{:S(2)}) async-start(bf16[16,40,8,128]{3,2,1,0:T(8,128)(2,1)} %bitcast.13), calls=%async_computation.1 | async-start | bytes 2621440 | tf_op jit(solution)/shard_map/all_to_all | solution.py:244
  335.9 0.0 copy-done.3
  335.9 18.8 %legendre_projection.2.refs_3_ = f32[40,2,2,32,320]{4,3,2,1,0:T(8,128)} custom-call(s32[40,2]{1,0:T(8,128)} %add_select_fusion.count_ref.refs_0_, bf16[16,40,8,128]{3,2,1,0:T(8,128)(2,1)} %copy-done, bf16[16,40,8,128]{3,2,1,0:T(8,128)(2,1)} %copy-done.1, bf16[16,40,8,128]{3,2,1,0:T(8,128)(2,1)} %copy-done.2, bf16[16,40,8,128]{3,2,1,0:T(8,128)(2,1)} %copy-done.3, ...), custom_call_target="tpu_custom_call" | custom-call | flops 1677721600 | bytes 32768000 | tf_op jit(solution)/shard_map/legendre_projection/pallas_call | solution.py:210
  354.8 11.7 %all-to-all-done.1.refs_1_ = bf16[16,40,8,128]{3,2,1,0:T(8,128)(2,1)S(1)} async-done(((bf16[16,40,8,128]{3,2,1,0:T(8,128)(2,1)}), bf16[16,40,8,128]{3,2,1,0:T(8,128)(2,1)S(1)}, u32[]{:S(2)}, u32[]{:S(2)}) %all-to-all-start.1) | async-done | bytes 1310752 | tf_op jit(solution)/shard_map/all_to_all | solution.py:244
  366.5 0.0 copy-start.4
  366.5 1.1 copy-done.4
  367.6 12.1 %legendre_projection.3 = f32[40,2,2,32,320]{4,3,2,1,0:T(8,128)} custom-call(s32[40,2]{1,0:T(8,128)} %add_select_fusion.count_ref.refs_0_, bf16[16,40,8,128]{3,2,1,0:T(8,128)(2,1)} %copy-done.4, bf16[40,2,320,640]{3,2,1,0:T(8,128)(2,1)} %refs_2_.1, f32[40,2,2,32,320]{4,3,2,1,0:T(8,128)} %legendre_projection.2.refs_3_), custom_call_target="tpu_custom_call", output_to_operand_aliasing={{}: (3, {})} | custom-call | flops 419430400 | bytes 13107200 | tf_op jit(solution)/shard_map/legendre_projection/pallas_call | solution.py:210
  (3 shorter events, 0.0 us)
Async XLA Ops:
  9.7 37.1 %all-to-all-start.8 = ((bf16[16,40,8,128]{3,2,1,0:T(8,128)(2,1)}), bf16[16,40,8,128]{3,2,1,0:T(8,128)(2,1)S(1)}, u32[]{:S(2)}, u32[]{:S(2)}) async-start(bf16[16,40,8,128]{3,2,1,0:T(8,128)(2,1)} %legendre_synthesis.9), calls=%async_computation.8 | async-start | bytes 2621440 | tf_op jit(solution)/shard_map/all_to_all | solution.py:244
  46.8 13.1 %copy-start.5 = (bf16[16,40,8,128]{3,2,1,0:T(8,128)(2,1)}, bf16[16,40,8,128]{3,2,1,0:T(8,128)(2,1)S(1)}, u32[]{:S(2)}) copy-start(bf16[16,40,8,128]{3,2,1,0:T(8,128)(2,1)S(1)} %all-to-all-done.8) | copy-start | bytes 3932164
  46.8 35.4 %all-to-all-start.6 = ((bf16[16,40,8,128]{3,2,1,0:T(8,128)(2,1)}), bf16[16,40,8,128]{3,2,1,0:T(8,128)(2,1)S(1)}, u32[]{:S(2)}, u32[]{:S(2)}) async-start(bf16[16,40,8,128]{3,2,1,0:T(8,128)(2,1)} %legendre_synthesis.8), calls=%async_computation.6 | async-start | bytes 2621440 | tf_op jit(solution)/shard_map/all_to_all | solution.py:244
  82.2 13.2 %copy-start.6 = (bf16[16,40,8,128]{3,2,1,0:T(8,128)(2,1)}, bf16[16,40,8,128]{3,2,1,0:T(8,128)(2,1)S(1)}, u32[]{:S(2)}) copy-start(bf16[16,40,8,128]{3,2,1,0:T(8,128)(2,1)S(1)} %all-to-all-done.6) | copy-start | bytes 3932164
  82.2 35.4 %all-to-all-start.4 = ((bf16[16,40,8,128]{3,2,1,0:T(8,128)(2,1)}), bf16[16,40,8,128]{3,2,1,0:T(8,128)(2,1)S(1)}, u32[]{:S(2)}, u32[]{:S(2)}) async-start(bf16[16,40,8,128]{3,2,1,0:T(8,128)(2,1)} %legendre_synthesis.7), calls=%async_computation.4 | async-start | bytes 2621440 | tf_op jit(solution)/shard_map/all_to_all | solution.py:244
  87.1 35.4 %copy-start.8 = (s32[640]{0:T(1024)S(1)}, s32[640]{0:T(1024)}, u32[]{:S(2)}) copy-start(s32[640]{0:T(1024)} %param.5) | copy-start | bytes 7684
  117.7 14.0 %copy-start.7 = (bf16[16,40,8,128]{3,2,1,0:T(8,128)(2,1)}, bf16[16,40,8,128]{3,2,1,0:T(8,128)(2,1)S(1)}, u32[]{:S(2)}) copy-start(bf16[16,40,8,128]{3,2,1,0:T(8,128)(2,1)S(1)} %all-to-all-done.4) | copy-start | bytes 3932164
  117.7 35.5 %all-to-all-start.2 = ((bf16[16,40,8,128]{3,2,1,0:T(8,128)(2,1)}), bf16[16,40,8,128]{3,2,1,0:T(8,128)(2,1)}, u32[]{:S(2)}, u32[]{:S(2)}) async-start(bf16[16,40,8,128]{3,2,1,0:T(8,128)(2,1)} %legendre_synthesis.6), calls=%async_computation.2 | async-start | bytes 2621440 | tf_op jit(solution)/shard_map/all_to_all | solution.py:244
  153.2 35.7 %all-to-all-start = ((bf16[16,40,8,128]{3,2,1,0:T(8,128)(2,1)}), bf16[16,40,8,128]{3,2,1,0:T(8,128)(2,1)}, u32[]{:S(2)}, u32[]{:S(2)}) async-start(bf16[16,40,8,128]{3,2,1,0:T(8,128)(2,1)} %legendre_synthesis.5), calls=%async_computation | async-start | bytes 2621440 | tf_op jit(solution)/shard_map/all_to_all | solution.py:244
  188.9 35.6 %all-to-all-start.3 = ((bf16[16,40,8,128]{3,2,1,0:T(8,128)(2,1)}), bf16[16,40,8,128]{3,2,1,0:T(8,128)(2,1)S(1)}, u32[]{:S(2)}, u32[]{:S(2)}) async-start(bf16[16,40,8,128]{3,2,1,0:T(8,128)(2,1)} %bitcast.15), calls=%async_computation.3 | async-start | bytes 2621440 | tf_op jit(solution)/shard_map/all_to_all | solution.py:244
  224.5 14.1 %copy-start = (bf16[16,40,8,128]{3,2,1,0:T(8,128)(2,1)}, bf16[16,40,8,128]{3,2,1,0:T(8,128)(2,1)S(1)}, u32[]{:S(2)}) copy-start(bf16[16,40,8,128]{3,2,1,0:T(8,128)(2,1)S(1)} %all-to-all-done.3.refs_1_) | copy-start | bytes 3932164
  224.5 35.4 %all-to-all-start.5 = ((bf16[16,40,8,128]{3,2,1,0:T(8,128)(2,1)}), bf16[16,40,8,128]{3,2,1,0:T(8,128)(2,1)S(1)}, u32[]{:S(2)}, u32[]{:S(2)}) async-start(bf16[16,40,8,128]{3,2,1,0:T(8,128)(2,1)} %bitcast.16), calls=%async_computation.5 | async-start | bytes 2621440 | tf_op jit(solution)/shard_map/all_to_all | solution.py:244
  260.0 14.5 %copy-start.1 = (bf16[16,40,8,128]{3,2,1,0:T(8,128)(2,1)}, bf16[16,40,8,128]{3,2,1,0:T(8,128)(2,1)S(1)}, u32[]{:S(2)}) copy-start(bf16[16,40,8,128]{3,2,1,0:T(8,128)(2,1)S(1)} %all-to-all-done.5.refs_2_) | copy-start | bytes 3932164
  260.0 35.7 %all-to-all-start.7 = ((bf16[16,40,8,128]{3,2,1,0:T(8,128)(2,1)}), bf16[16,40,8,128]{3,2,1,0:T(8,128)(2,1)S(1)}, u32[]{:S(2)}, u32[]{:S(2)}) async-start(bf16[16,40,8,128]{3,2,1,0:T(8,128)(2,1)} %bitcast.17), calls=%async_computation.7 | async-start | bytes 2621440 | tf_op jit(solution)/shard_map/all_to_all | solution.py:244
  295.6 14.1 %copy-start.2 = (bf16[16,40,8,128]{3,2,1,0:T(8,128)(2,1)}, bf16[16,40,8,128]{3,2,1,0:T(8,128)(2,1)S(1)}, u32[]{:S(2)}) copy-start(bf16[16,40,8,128]{3,2,1,0:T(8,128)(2,1)S(1)} %all-to-all-done.7.refs_3_) | copy-start | bytes 3932164
  295.6 35.4 %all-to-all-start.9 = ((bf16[16,40,8,128]{3,2,1,0:T(8,128)(2,1)}), bf16[16,40,8,128]{3,2,1,0:T(8,128)(2,1)S(1)}, u32[]{:S(2)}, u32[]{:S(2)}) async-start(bf16[16,40,8,128]{3,2,1,0:T(8,128)(2,1)} %bitcast.14), calls=%async_computation.9 | async-start | bytes 2621440 | tf_op jit(solution)/shard_map/all_to_all | solution.py:244
  331.1 4.9 %copy-start.3 = (bf16[16,40,8,128]{3,2,1,0:T(8,128)(2,1)}, bf16[16,40,8,128]{3,2,1,0:T(8,128)(2,1)S(1)}, u32[]{:S(2)}) copy-start(bf16[16,40,8,128]{3,2,1,0:T(8,128)(2,1)S(1)} %all-to-all-done.9.refs_4_) | copy-start | bytes 3932164
  331.1 35.4 %all-to-all-start.1 = ((bf16[16,40,8,128]{3,2,1,0:T(8,128)(2,1)}), bf16[16,40,8,128]{3,2,1,0:T(8,128)(2,1)S(1)}, u32[]{:S(2)}, u32[]{:S(2)}) async-start(bf16[16,40,8,128]{3,2,1,0:T(8,128)(2,1)} %bitcast.13), calls=%async_computation.1 | async-start | bytes 2621440 | tf_op jit(solution)/shard_map/all_to_all | solution.py:244
  366.5 1.1 copy-start.4

commit v2 on v1

--- a/solution.py
+++ b/solution.py
@@ -15,6 +15,8 @@
 XBLOCK = 256
 SBLOCK = 128
 VMEM = 56 << 20
+FORWARD = (1, 4)
+RETURN = ((0, 0, 1), (1, 0, 3), (1, 3, 1))
 
 
 def quarter_sine(t):
@@ -57,7 +59,7 @@
 
 
 def synthesis_kernel(count_ref, spectral_ref, legendre_ref, out_ref, scratch):
-    step = pl.program_id(0)
+    step = pl.program_id(1)
     levels = out_ref.shape[0] // 2
     rows = spectral_ref.shape[2] * spectral_ref.shape[3]
     half = spectral_ref.shape[4]
@@ -74,10 +76,10 @@
         for v in range(levels):
             for ns in range(2):
                 tile = scratch[s, ns, pl.ds(v, rows // levels, stride=levels), :]
-                out_ref[2 * v + ns, s] = tile.astype(jnp.bfloat16)
-
-
-def synthesize(counts, spectral, legendre, chunk):
+                out_ref[2 * v + ns, 0, s] = tile.astype(jnp.bfloat16)
+
+
+def synthesize(counts, spectral, legendre, units):
     slots, _, _, slabs, half = spectral.shape
     levels = slabs // FIELDS
     rows = 2 * FIELDS
@@ -85,15 +87,15 @@
         synthesis_kernel,
         grid_spec=pltpu.PrefetchScalarGridSpec(
             num_scalar_prefetch=1,
-            grid=(slots // SLOTS_PER_STEP,),
+            grid=(len(units), slots // SLOTS_PER_STEP),
             in_specs=[
-                pl.BlockSpec((SLOTS_PER_STEP, 2, 2, slabs, half), lambda i, c: (i, 0, 0, 0, 0)),
-                pl.BlockSpec((SLOTS_PER_STEP, 2, half, LANES), lambda i, c: (i, 0, 0, chunk)),
+                pl.BlockSpec((SLOTS_PER_STEP, 2, 2, slabs, half), lambda u, i, c: (i, 0, 0, 0, 0)),
+                pl.BlockSpec((SLOTS_PER_STEP, 2, half, LANES), lambda u, i, c: (i, 0, 0, units[0] + u)),
             ],
-            out_specs=pl.BlockSpec((2 * levels, SLOTS_PER_STEP, rows, LANES), lambda i, c: (0, i, 0, 0)),
+            out_specs=pl.BlockSpec((2 * levels, 1, SLOTS_PER_STEP, rows, LANES), lambda u, i, c: (0, u, i, 0, 0)),
             scratch_shapes=[pltpu.VMEM((SLOTS_PER_STEP, 2, 2 * slabs, LANES), jnp.float32)],
         ),
-        out_shape=jax.ShapeDtypeStruct((2 * levels, slots, rows, LANES), jnp.bfloat16),
+        out_shape=jax.ShapeDtypeStruct((2 * levels, len(units), slots, rows, LANES), jnp.bfloat16),
         compiler_params=pltpu.CompilerParams(vmem_limit_bytes=VMEM),
         cost_estimate=pl.CostEstimate(
             flops=2 * slots * 2 * 2 * slabs * half * LANES,
@@ -105,9 +107,8 @@
 
 
 def grid_kernel(y_ref, sc_ref, ss_ref, ac_ref, as_ref, alt_ref, out_ref, wide, cos_in, sin_in, even, odd):
-    waves = y_ref.shape[0]
-    rows = y_ref.shape[1]
-    width = FIELDS * LANES
+    ranks, _, slots, rows, _ = y_ref.shape
+    waves = ranks * slots
     wide[...] = y_ref[...].reshape(waves * rows, LANES).astype(jnp.float32)
     for f in range(FIELDS):
         columns = pl.ds(f * LANES, LANES)
@@ -128,23 +129,28 @@
     middle = (middle * partner(middle)).astype(jnp.bfloat16).astype(jnp.float32)[0:1, :]
 
     for b in range(waves // SBLOCK):
-        slots = pl.ds(b * SBLOCK, SBLOCK)
-        cos_out = jnp.dot(ac_ref[slots, :], even[...], preferred_element_type=jnp.float32)
-        cos_out = cos_out + alt_ref[slots, :] * middle
-        sin_out = jnp.dot(as_ref[slots, :], odd[...], preferred_element_type=jnp.float32)
+        part = pl.ds(b * SBLOCK, SBLOCK)
+        cos_out = jnp.dot(ac_ref[part, :], even[...], preferred_element_type=jnp.float32)
+        cos_out = cos_out + alt_ref[part, :] * middle
+        sin_out = jnp.dot(as_ref[part, :], odd[...], preferred_element_type=jnp.float32)
         for f in range(FIELDS):
             columns = slice(f * LANES, (f + 1) * LANES)
             wide[pl.ds(b * SBLOCK * rows + f, SBLOCK, stride=rows), :] = cos_out[:, columns]
             wide[pl.ds(b * SBLOCK * rows + FIELDS + f, SBLOCK, stride=rows), :] = sin_out[:, columns]
-    out_ref[...] = wide[...].astype(jnp.bfloat16).reshape(waves, rows, LANES)
-
-
-def grid_product(y, tables):
-    waves, rows, _ = y.shape
+    out_ref[...] = wide[...].astype(jnp.bfloat16).reshape(ranks, 1, slots, rows, LANES)
+
+
+def grid_product(y, tables, first, units):
+    ranks, _, slots, rows, _ = y.shape
+    waves = ranks * slots
     width = FIELDS * LANES
     return pl.pallas_call(
         grid_kernel,
-        out_shape=jax.ShapeDtypeStruct(y.shape, jnp.bfloat16),
+        grid=(units,),
+        in_specs=[pl.BlockSpec((ranks, 1, slots, rows, LANES), lambda u: (0, first + u, 0, 0, 0))]
+        + [pl.BlockSpec(t.shape, lambda u: (0, 0)) for t in tables],
+        out_specs=pl.BlockSpec((ranks, 1, slots, rows, LANES), lambda u: (0, u, 0, 0, 0)),
+        out_shape=jax.ShapeDtypeStruct((ranks, units, slots, rows, LANES), jnp.bfloat16),
         scratch_shapes=[
             pltpu.VMEM((waves * rows, LANES), jnp.float32),
             pltpu.VMEM((waves, width), jnp.bfloat16),
@@ -154,20 +160,24 @@
         ],
         compiler_params=pltpu.CompilerParams(vmem_limit_bytes=VMEM),
         cost_estimate=pl.CostEstimate(
-            flops=8 * waves * HALF * width, transcendentals=0, bytes_accessed=8 * waves * HALF + 4 * waves * rows * LANES
+            flops=units * 8 * waves * HALF * width,
+            transcendentals=0,
+            bytes_accessed=8 * waves * HALF + units * 4 * waves * rows * LANES,
         ),
         name="grid_product",
     )(y, *tables)
 
 
-def projection_kernel(chunks, added, count_ref, *refs):
-    arrived = refs[:chunks]
-    legendres = refs[chunks : 2 * chunks]
-    before = refs[2 * chunks] if added else None
+def projection_kernel(sizes, added, count_ref, *refs):
+    chunks = sum(sizes)
+    arrived = refs[: len(sizes)]
+    legendres = refs[len(sizes) : len(sizes) + chunks]
+    before = refs[len(sizes) + chunks] if added else None
+    homes = [(arrived[c], u) for c in range(len(sizes)) for u in range(sizes[c])]
     out_ref, scratch = refs[-2], refs[-1]
     step = pl.program_id(0)
     levels = arrived[0].shape[0] // 2
-    fields = arrived[0].shape[2]
+    fields = arrived[0].shape[3]
     rows = levels * fields
     half = legendres[0].shape[2]
     lane = lax.broadcasted_iota(jnp.int32, (rows, half), 1)
@@ -175,8 +185,9 @@
         sums = [None, None]
         for k in range(chunks):
             for v in range(levels):
-                north = arrived[k][2 * v, s].astype(jnp.float32)
-                south = arrived[k][2 * v + 1, s].astype(jnp.float32)
+                ref, u = homes[k]
+                north = ref[2 * v, u, s].astype(jnp.float32)
+                south = ref[2 * v + 1, u, s].astype(jnp.float32)
                 scratch[s, k, 0, pl.ds(v * fields, fields), :] = north + south
                 scratch[s, k, 1, pl.ds(v * fields, fields), :] = north - south
             for p in range(2):
@@ -196,8 +207,9 @@
 
 
 def project(counts, arrived, legendre, chunk_ids, before=None):
-    chunks = len(arrived)
-    ranks, slots, fields, _ = arrived[0].shape
+    sizes = [a.shape[1] for a in arrived]
+    chunks = len(chunk_ids)
+    ranks, _, slots, fields, _ = arrived[0].shape
     slabs = ranks // 2 * FIELDS
     half = legendre.shape[2]
     n = SLOTS_PER_STEP
@@ -205,21 +217,21 @@
     added = before is not None
 
     def kernel(*refs):
-        projection_kernel(chunks, added, *refs)
+        projection_kernel(sizes, added, *refs)
 
     return pl.pallas_call(
         kernel,
         grid_spec=pltpu.PrefetchScalarGridSpec(
             num_scalar_prefetch=1,
             grid=(slots // n,),
-            in_specs=[pl.BlockSpec((ranks, n, fields, LANES), lambda i, c: (0, i, 0, 0))] * chunks
+            in_specs=[pl.BlockSpec((ranks, size, n, fields, LANES), lambda i, c: (0, 0, i, 0, 0)) for size in sizes]
             + [pl.BlockSpec((n, 2, half, LANES), lambda i, c, k=k: (i, 0, 0, k)) for k in chunk_ids]
             + ([out_spec] if added else []),
             out_specs=out_spec,
             scratch_shapes=[pltpu.VMEM((n, chunks, 2, 2 * slabs, LANES), jnp.float32)],
         ),
         out_shape=jax.ShapeDtypeStruct((slots, 2, 2, slabs, half), jnp.float32),
-        input_output_aliases={1 + 2 * chunks: 0} if added else {},
+        input_output_aliases={1 + len(sizes) + chunks: 0} if added else {},
         compiler_params=pltpu.CompilerParams(vmem_limit_bytes=VMEM),
         cost_estimate=pl.CostEstimate(
             flops=2 * chunks * slots * 2 * 2 * slabs * half * LANES,
@@ -234,7 +246,6 @@
     slots, _, _, slabs, half = spectral_in.shape
     total = wave_of_slot.shape[0]
     ranks = total // slots
-    chunks = legendre.shape[3] // LANES
     start = lax.axis_index("lat") * slots
     own = lax.dynamic_slice_in_dim(wave_of_slot, start, slots)
     counts = (total + 1 - own[:, None] - jnp.arange(2, dtype=jnp.int32)[None, :]) // 2
@@ -243,13 +254,15 @@
     def exchange(x):
         return lax.all_to_all(x, "lat", split_axis=0, concat_axis=0, tiled=True)
 
-    sent = [exchange(synthesize(counts, spectral_in, legendre, k)) for k in range(chunks)]
-    back = []
-    for y in sent:
-        product = grid_product(y.reshape(total, 2 * FIELDS, LANES), tables)
-        back.append(exchange(product.reshape(ranks, slots, 2 * FIELDS, LANES)))
-    first = project(counts, back[:-1], legendre, range(chunks - 1))
-    return project(counts, back[-1:], legendre, [chunks - 1], first)
+    sent, at = [], 0
+    for size in FORWARD:
+        sent.append(exchange(synthesize(counts, spectral_in, legendre, range(at, at + size))))
+        at += size
+    back = [exchange(grid_product(sent[c], tables, first, units)) for c, first, units in RETURN]
+    places = [sum(FORWARD[:c]) + first for c, first, _ in RETURN]
+    ids = [list(range(p, p + r[2])) for p, r in zip(places, RETURN)]
+    sums = project(counts, back[:-1], legendre, [k for i in ids[:-1] for k in i])
+    return project(counts, back[-1:], legendre, ids[-1], sums)
 
 
 def basis_tables(wave_of_slot):
@@ -295,7 +308,7 @@
 
     def local(spectral_in, legendre, wave_of_slot):
         slots, _, _, slabs, _ = spectral_in.shape
-        whole_tiles = slots % SLOTS_PER_STEP == 0 and legendre.shape[3] % LANES == 0
+        whole_tiles = slots % SLOTS_PER_STEP == 0 and legendre.shape[3] == sum(FORWARD) * LANES
         if rows * FIELDS == 2 * slabs and whole_tiles and wave_of_slot.shape[0] % SBLOCK == 0:
             return per_device(spectral_in, legendre, wave_of_slot)
         return per_device_general(spectral_in, legendre, wave_of_slot)

time: 386 us -> 346 us (0.90); the launches traced: 380 us -> 345 us
  starting transfers between devices: 51.3 us -> 26.1 us
  Pallas kernels: 119 us -> 102 us
  waiting for transfers between devices: 192 us -> 197 us
    all_to_all x10 -> x5, starting transfers between devices: 51.3 us -> 26.1 us  [exchange(): return lax.all_to_all(x, 'lat', split_axis=0, concat_axis=0, tiled=True)]
    pallas_call x5 -> x3, Pallas kernels: 46.3 us -> 37.4 us  [grid_product(): pl.pallas_call(grid_kernel, grid=(units,), in_specs=[pl.BlockSpec((ranks,...]
    pallas_call x5 -> x2, Pallas kernels: 41.3 us -> 33.3 us  [synthesize(): pl.pallas_call(synthesis_kernel, grid_spec=pltpu.PrefetchScalarGridSpec(n...]
    all_to_all x10 -> x5, waiting for transfers between devices: 192 us -> 197 us  [exchange(): return lax.all_to_all(x, 'lat', split_axis=0, concat_axis=0, tiled=True)]
  transfers between devices with their start and end apart: 10 -> 5, of which waited for: 10 -> 5; matrix products, arithmetic and copies ran while one was open for 4% -> 4% of each run, Pallas kernels for 26% -> 24%
where the time goes in v2:
time: 346 us; the launch traced here: 345 us
  waiting for transfers between devices  197 us (57%)
  Pallas kernels  102 us (29%)
  starting transfers between devices  26.1 us (8%)
  other arithmetic  15.5 us (4%)
  local copies, waits for them, and re-layouts  4.14 us (1%)
    all_to_all x5, waiting for transfers between devices, exchange(): return lax.all_to_all(x, 'lat', split_axis=0, concat_axis=0, tiled=True)  197 us
    pallas_call x3, Pallas kernels, grid_product(): pl.pallas_call(grid_kernel, grid=(units,), in_specs=[pl.BlockSpec((ranks,...  37.4 us
    pallas_call x2, Pallas kernels, synthesize(): pl.pallas_call(synthesis_kernel, grid_spec=pltpu.PrefetchScalarGridSpec(n...  33.3 us
    pallas_call x2, Pallas kernels, project(): pl.pallas_call(kernel, grid_spec=pltpu.PrefetchScalarGridSpec(num_scalar_...  30.9 us
    all_to_all x5, starting transfers between devices, exchange(): return lax.all_to_all(x, 'lat', split_axis=0, concat_axis=0, tiled=True)  26.1 us
  transfers between devices with their start and end apart: 5, of which 5 were waited for; matrix products, arithmetic and copies ran while one was open for 4% of the time, Pallas kernels for 24%

profile of v2, /device:TPU:13, one launch (start us, length us, event | category | flops | bytes accessed | tf_op | source)
XLA Modules:
  0.0 344.7 jit_solution(16895458193786472018)
XLA Ops:
  0.0 0.8 dynamic-slice_subtract_fusion
  0.8 0.7 add_select_fusion.count_ref.refs_0_
  1.4 8.3 %legendre_synthesis.3 = bf16[16,1,40,8,128]{4,3,2,1,0:T(8,128)(2,1)} custom-call(s32[40,2]{1,0:T(8,128)} %add_select_fusion.count_ref.refs_0_, bf16[40,2,2,32,320]{4,3,2,1,0:T(8,128)(2,1)} %spectral_ref.3, bf16[40,2,320,640]{3,2,1,0:T(8,128)(2,1)} %refs_2_.1), custom_call_target="tpu_custom_call" | custom-call | flops 419430400 | bytes 9830400 | tf_op jit(solution)/shard_map/legendre_synthesis/pallas_call | solution.py:86
  9.7 6.6 %all-to-all-start.2 = ((bf16[16,1,40,8,128]{4,3,2,1,0:T(8,128)(2,1)}), bf16[16,1,40,8,128]{4,3,2,1,0:T(8,128)(2,1)S(1)}, u32[]{:S(2)}, u32[]{:S(2)}) async-start(bf16[16,1,40,8,128]{4,3,2,1,0:T(8,128)(2,1)} %legendre_synthesis.3), calls=%async_computation.2 | async-start | bytes 2621440 | tf_op jit(solution)/shard_map/all_to_all | solution.py:255
  16.3 25.1 %legendre_synthesis.2 = bf16[16,4,40,8,128]{4,3,2,1,0:T(8,128)(2,1)} custom-call(s32[40,2]{1,0:T(8,128)} %add_select_fusion.count_ref.refs_0_, bf16[40,2,2,32,320]{4,3,2,1,0:T(8,128)(2,1)} %spectral_ref.3, bf16[40,2,320,640]{3,2,1,0:T(8,128)(2,1)} %refs_2_.1), custom_call_target="tpu_custom_call" | custom-call | flops 419430400 | bytes 9830400 | tf_op jit(solution)/shard_map/legendre_synthesis/pallas_call | solution.py:86
  41.4 0.0 copy-start.3
  41.4 5.5 %all-to-all-done.2.y_ref = bf16[16,1,40,8,128]{4,3,2,1,0:T(8,128)(2,1)S(1)} async-done(((bf16[16,1,40,8,128]{4,3,2,1,0:T(8,128)(2,1)}), bf16[16,1,40,8,128]{4,3,2,1,0:T(8,128)(2,1)S(1)}, u32[]{:S(2)}, u32[]{:S(2)}) %all-to-all-start.2) | async-done | bytes 1310752 | tf_op jit(solution)/shard_map/all_to_all | solution.py:255
  46.8 0.0 copy-start.2
  46.8 1.1 copy-done.2
  48.0 4.9 %all-to-all-start = ((bf16[16,4,40,8,128]{4,3,2,1,0:T(8,128)(2,1)}), bf16[16,4,40,8,128]{4,3,2,1,0:T(8,128)(2,1)}, u32[]{:S(2)}, u32[]{:S(2)}) async-start(bf16[16,4,40,8,128]{4,3,2,1,0:T(8,128)(2,1)} %legendre_synthesis.2), calls=%async_computation | async-start | bytes 10485760 | tf_op jit(solution)/shard_map/all_to_all | solution.py:255
  52.8 0.0 copy-done.3
  52.9 0.9 reshape.8.alt_ref
  53.7 3.6 %multiply_subtract_fusion.1 = (f32[1296,640]{1,0:T(8,128)S(1)}, bf16[1296,640]{1,0:T(8,128)(2,1)}) fusion(f32[640]{0:T(1024)S(1)} %convert_element_type.19, f32[640]{0:T(1024)S(1)} %get-tuple-element.8), kind=kLoop, calls=%fused_computation.11 | loop fusion | flops 18247680 | bytes 4981760 | tf_op jit(solution)/shard_map/sub | solution.py:32
  57.4 4.0 %multiply_convert_fusion.2.ss_ref = bf16[1280,640]{1,0:T(8,128)(2,1)} fusion(f32[1296,640]{1,0:T(8,128)S(1)} %get-tuple-element.9, f32[640]{0:T(1024)S(1)} %get-tuple-element.8), kind=kLoop, calls=%fused_computation.37 | loop fusion | flops 17203200 | bytes 4917760 | tf_op jit(solution)/shard_map/convert_element_type | solution.py:51
  61.4 6.4 %fusion.13 = (bf16[640,1280]{1,0:T(8,128)(2,1)}, bf16[640,1280]{1,0:T(8,128)(2,1)}) fusion(f32[1280]{0:T(1024)S(1)} %get-tuple-element.12, f32[1280]{0:T(1024)S(1)} %get-tuple-element.11, f32[640]{0:T(1024)S(1)} %convert_element_type.19), kind=kLoop, calls=%fused_computation.22 | loop fusion | flops 34406400 | bytes 3289600 | tf_op jit(solution)/shard_map/convert_element_type | solution.py:56
  67.8 9.2 %grid_product.4 = bf16[16,1,40,8,128]{4,3,2,1,0:T(8,128)(2,1)} custom-call(bf16[16,1,40,8,128]{4,3,2,1,0:T(8,128)(2,1)} %copy-done.2, bf16[1296,640]{1,0:T(8,128)(2,1)} %get-tuple-element.10.sc_ref, bf16[1280,640]{1,0:T(8,128)(2,1)} %multiply_convert_fusion.2.ss_ref, bf16[640,1280]{1,0:T(8,128)(2,1)} %get-tuple-element.6.ac_ref, ...), custom_call_target="tpu_custom_call" | custom-call | flops 3355443200 | bytes 9175040 | tf_op jit(solution)/shard_map/grid_product/pallas_call | solution.py:147
  77.0 90.7 %all-to-all-done.y_ref = bf16[16,4,40,8,128]{4,3,2,1,0:T(8,128)(2,1)} async-done(((bf16[16,4,40,8,128]{4,3,2,1,0:T(8,128)(2,1)}), bf16[16,4,40,8,128]{4,3,2,1,0:T(8,128)(2,1)}, u32[]{:S(2)}, u32[]{:S(2)}) %all-to-all-start) | async-done | bytes 5242912 | tf_op jit(solution)/shard_map/all_to_all | solution.py:255
  167.8 4.9 %all-to-all-start.3 = ((bf16[16,1,40,8,128]{4,3,2,1,0:T(8,128)(2,1)}), bf16[16,1,40,8,128]{4,3,2,1,0:T(8,128)(2,1)S(1)}, u32[]{:S(2)}, u32[]{:S(2)}) async-start(bf16[16,1,40,8,128]{4,3,2,1,0:T(8,128)(2,1)} %grid_product.4), calls=%async_computation.3 | async-start | bytes 2621440 | tf_op jit(solution)/shard_map/all_to_all | solution.py:255
  172.7 18.9 %grid_product.5 = bf16[16,3,40,8,128]{4,3,2,1,0:T(8,128)(2,1)} custom-call(bf16[16,4,40,8,128]{4,3,2,1,0:T(8,128)(2,1)} %all-to-all-done.y_ref, bf16[1296,640]{1,0:T(8,128)(2,1)} %get-tuple-element.10.sc_ref, bf16[1280,640]{1,0:T(8,128)(2,1)} %multiply_convert_fusion.2.ss_ref, bf16[640,1280]{1,0:T(8,128)(2,1)} %get-tuple-element.6.ac_ref, ...), custom_call_target="tpu_custom_call" | custom-call | flops 10066329600 | bytes 14417920 | tf_op jit(solution)/shard_map/grid_product/pallas_call | solution.py:147
  191.5 11.7 %all-to-all-done.3.refs_1_ = bf16[16,1,40,8,128]{4,3,2,1,0:T(8,128)(2,1)S(1)} async-done(((bf16[16,1,40,8,128]{4,3,2,1,0:T(8,128)(2,1)}), bf16[16,1,40,8,128]{4,3,2,1,0:T(8,128)(2,1)S(1)}, u32[]{:S(2)}, u32[]{:S(2)}) %all-to-all-start.3) | async-done | bytes 1310752 | tf_op jit(solution)/shard_map/all_to_all | solution.py:255
  203.2 0.0 copy-start
  203.2 1.1 copy-done
  204.3 4.9 %all-to-all-start.4 = ((bf16[16,3,40,8,128]{4,3,2,1,0:T(8,128)(2,1)}), bf16[16,3,40,8,128]{4,3,2,1,0:T(8,128)(2,1)}, u32[]{:S(2)}, u32[]{:S(2)}) async-start(bf16[16,3,40,8,128]{4,3,2,1,0:T(8,128)(2,1)} %grid_product.5), calls=%async_computation.4 | async-start | bytes 7864320 | tf_op jit(solution)/shard_map/all_to_all | solution.py:255
  209.2 9.2 %grid_product.3 = bf16[16,1,40,8,128]{4,3,2,1,0:T(8,128)(2,1)} custom-call(bf16[16,4,40,8,128]{4,3,2,1,0:T(8,128)(2,1)} %all-to-all-done.y_ref, bf16[1296,640]{1,0:T(8,128)(2,1)} %get-tuple-element.10.sc_ref, bf16[1280,640]{1,0:T(8,128)(2,1)} %multiply_convert_fusion.2.ss_ref, bf16[640,1280]{1,0:T(8,128)(2,1)} %get-tuple-element.6.ac_ref, ...), custom_call_target="tpu_custom_call" | custom-call | flops 3355443200 | bytes 9175040 | tf_op jit(solution)/shard_map/grid_product/pallas_call | solution.py:147
  218.4 77.6 %all-to-all-done.4.refs_2_ = bf16[16,3,40,8,128]{4,3,2,1,0:T(8,128)(2,1)} async-done(((bf16[16,3,40,8,128]{4,3,2,1,0:T(8,128)(2,1)}), bf16[16,3,40,8,128]{4,3,2,1,0:T(8,128)(2,1)}, u32[]{:S(2)}, u32[]{:S(2)}) %all-to-all-start.4) | async-done | bytes 3932192 | tf_op jit(solution)/shard_map/all_to_all | solution.py:255
  296.0 4.9 %all-to-all-start.1 = ((bf16[16,1,40,8,128]{4,3,2,1,0:T(8,128)(2,1)}), bf16[16,1,40,8,128]{4,3,2,1,0:T(8,128)(2,1)S(1)}, u32[]{:S(2)}, u32[]{:S(2)}) async-start(bf16[16,1,40,8,128]{4,3,2,1,0:T(8,128)(2,1)} %grid_product.3), calls=%async_computation.1 | async-start | bytes 2621440 | tf_op jit(solution)/shard_map/all_to_all | solution.py:255
  300.9 18.8 %legendre_projection.2.refs_3_ = f32[40,2,2,32,320]{4,3,2,1,0:T(8,128)} custom-call(s32[40,2]{1,0:T(8,128)} %add_select_fusion.count_ref.refs_0_, bf16[16,1,40,8,128]{4,3,2,1,0:T(8,128)(2,1)} %copy-done, bf16[16,3,40,8,128]{4,3,2,1,0:T(8,128)(2,1)} %all-to-all-done.4.refs_2_, bf16[40,2,320,640]{3,2,1,0:T(8,128)(2,1)} %refs_2_.1, ...), custom_call_target="tpu_custom_call" | custom-call | flops 1677721600 | bytes 32768000 | tf_op jit(solution)/shard_map/legendre_projection/pallas_call | solution.py:222
  319.8 11.7 %all-to-all-done.1.refs_1_ = bf16[16,1,40,8,128]{4,3,2,1,0:T(8,128)(2,1)S(1)} async-done(((bf16[16,1,40,8,128]{4,3,2,1,0:T(8,128)(2,1)}), bf16[16,1,40,8,128]{4,3,2,1,0:T(8,128)(2,1)S(1)}, u32[]{:S(2)}, u32[]{:S(2)}) %all-to-all-start.1) | async-done | bytes 1310752 | tf_op jit(solution)/shard_map/all_to_all | solution.py:255
  331.5 0.0 copy-start.1
  331.5 1.1 copy-done.1
  332.6 12.1 %legendre_projection.3 = f32[40,2,2,32,320]{4,3,2,1,0:T(8,128)} custom-call(s32[40,2]{1,0:T(8,128)} %add_select_fusion.count_ref.refs_0_, bf16[16,1,40,8,128]{4,3,2,1,0:T(8,128)(2,1)} %copy-done.1, bf16[40,2,320,640]{3,2,1,0:T(8,128)(2,1)} %refs_2_.1, f32[40,2,2,32,320]{4,3,2,1,0:T(8,128)} %legendre_projection.2.refs_3_), custom_call_target="tpu_custom_call", output_to_operand_aliasing={{}: (3, {})} | custom-call | flops 419430400 | bytes 13107200 | tf_op jit(solution)/shard_map/legendre_projection/pallas_call | solution.py:222
  (3 shorter events, 0.0 us)
Async XLA Ops:
  9.7 37.1 %all-to-all-start.2 = ((bf16[16,1,40,8,128]{4,3,2,1,0:T(8,128)(2,1)}), bf16[16,1,40,8,128]{4,3,2,1,0:T(8,128)(2,1)S(1)}, u32[]{:S(2)}, u32[]{:S(2)}) async-start(bf16[16,1,40,8,128]{4,3,2,1,0:T(8,128)(2,1)} %legendre_synthesis.3), calls=%async_computation.2 | async-start | bytes 2621440 | tf_op jit(solution)/shard_map/all_to_all | solution.py:255
  41.4 11.5 %copy-start.3 = (s32[640]{0:T(1024)S(1)}, s32[640]{0:T(1024)}, u32[]{:S(2)}) copy-start(s32[640]{0:T(1024)} %param.5) | copy-start | bytes 7684
  46.8 1.1 copy-start.2
  48.0 119.8 %all-to-all-start = ((bf16[16,4,40,8,128]{4,3,2,1,0:T(8,128)(2,1)}), bf16[16,4,40,8,128]{4,3,2,1,0:T(8,128)(2,1)}, u32[]{:S(2)}, u32[]{:S(2)}) async-start(bf16[16,4,40,8,128]{4,3,2,1,0:T(8,128)(2,1)} %legendre_synthesis.2), calls=%async_computation | async-start | bytes 10485760 | tf_op jit(solution)/shard_map/all_to_all | solution.py:255
  167.8 35.5 %all-to-all-start.3 = ((bf16[16,1,40,8,128]{4,3,2,1,0:T(8,128)(2,1)}), bf16[16,1,40,8,128]{4,3,2,1,0:T(8,128)(2,1)S(1)}, u32[]{:S(2)}, u32[]{:S(2)}) async-start(bf16[16,1,40,8,128]{4,3,2,1,0:T(8,128)(2,1)} %grid_product.4), calls=%async_computation.3 | async-start | bytes 2621440 | tf_op jit(solution)/shard_map/all_to_all | solution.py:255
  203.2 1.1 copy-start
  204.3 91.7 %all-to-all-start.4 = ((bf16[16,3,40,8,128]{4,3,2,1,0:T(8,128)(2,1)}), bf16[16,3,40,8,128]{4,3,2,1,0:T(8,128)(2,1)}, u32[]{:S(2)}, u32[]{:S(2)}) async-start(bf16[16,3,40,8,128]{4,3,2,1,0:T(8,128)(2,1)} %grid_product.5), calls=%async_computation.4 | async-start | bytes 7864320 | tf_op jit(solution)/shard_map/all_to_all | solution.py:255
  296.0 35.5 %all-to-all-start.1 = ((bf16[16,1,40,8,128]{4,3,2,1,0:T(8,128)(2,1)}), bf16[16,1,40,8,128]{4,3,2,1,0:T(8,128)(2,1)S(1)}, u32[]{:S(2)}, u32[]{:S(2)}) async-start(bf16[16,1,40,8,128]{4,3,2,1,0:T(8,128)(2,1)} %grid_product.3), calls=%async_computation.1 | async-start | bytes 2621440 | tf_op jit(solution)/shard_map/all_to_all | solution.py:255
  331.5 1.1 copy-start.1

commit v3 on v2

--- a/solution.py
+++ b/solution.py
@@ -11,7 +11,7 @@
 FIELDS = 4
 HALF = NLON // 2
 LANES = 128
-SLOTS_PER_STEP = 8
+SLOTS_PER_STEP = 20
 XBLOCK = 256
 SBLOCK = 128
 VMEM = 56 << 20

time: 346 us -> 342 us (0.988)
  Pallas kernels: 102 us -> 90.8 us
  waiting for transfers between devices: 197 us -> 204 us
    pallas_call x2, Pallas kernels: 33.3 us -> 25.9 us  [synthesize(): pl.pallas_call(synthesis_kernel, grid_spec=pltpu.PrefetchScalarGridSpec(n...]
    all_to_all x5, waiting for transfers between devices: 197 us -> 204 us  [exchange(): return lax.all_to_all(x, 'lat', split_axis=0, concat_axis=0, tiled=True)]
  transfers between devices with their start and end apart: 5 -> 5, of which waited for: 5 -> 5; matrix products, arithmetic and copies ran while one was open for 4% -> 4% of each run, Pallas kernels for 24% -> 22%
where the time goes in v3:
time: 342 us; the launch traced here: 341 us
  waiting for transfers between devices  204 us (60%)
  Pallas kernels  90.8 us (27%)
  starting transfers between devices  26.1 us (8%)
  other arithmetic  15.5 us (5%)
  local copies, waits for them, and re-layouts  4.14 us (1%)
    all_to_all x5, waiting for transfers between devices, exchange(): return lax.all_to_all(x, 'lat', split_axis=0, concat_axis=0, tiled=True)  204 us
    pallas_call x3, Pallas kernels, grid_product(): pl.pallas_call(grid_kernel, grid=(units,), in_specs=[pl.BlockSpec((ranks,...  37.4 us
    pallas_call x2, Pallas kernels, project(): pl.pallas_call(kernel, grid_spec=pltpu.PrefetchScalarGridSpec(num_scalar_...  27.6 us
    all_to_all x5, starting transfers between devices, exchange(): return lax.all_to_all(x, 'lat', split_axis=0, concat_axis=0, tiled=True)  26.1 us
    pallas_call x2, Pallas kernels, synthesize(): pl.pallas_call(synthesis_kernel, grid_spec=pltpu.PrefetchScalarGridSpec(n...  25.9 us
  transfers between devices with their start and end apart: 5, of which 5 were waited for; matrix products, arithmetic and copies ran while one was open for 4% of the time, Pallas kernels for 22%

profile of v3, /device:TPU:13, one launch (start us, length us, event | category | flops | bytes accessed | tf_op | source)
XLA Modules:
  0.0 341.0 jit_solution(13299140936538118860)
XLA Ops:
  0.0 0.8 dynamic-slice_subtract_fusion
  0.8 0.7 add_select_fusion.count_ref.refs_0_
  1.4 6.9 %legendre_synthesis.3 = bf16[16,1,40,8,128]{4,3,2,1,0:T(8,128)(2,1)} custom-call(s32[40,2]{1,0:T(8,128)} %add_select_fusion.count_ref.refs_0_, bf16[40,2,2,32,320]{4,3,2,1,0:T(8,128)(2,1)} %spectral_ref.3, bf16[40,2,320,640]{3,2,1,0:T(8,128)(2,1)} %refs_2_.1), custom_call_target="tpu_custom_call" | custom-call | flops 419430400 | bytes 9830400 | tf_op jit(solution)/shard_map/legendre_synthesis/pallas_call | solution.py:86
  8.3 6.6 %all-to-all-start.2 = ((bf16[16,1,40,8,128]{4,3,2,1,0:T(8,128)(2,1)}), bf16[16,1,40,8,128]{4,3,2,1,0:T(8,128)(2,1)S(1)}, u32[]{:S(2)}, u32[]{:S(2)}) async-start(bf16[16,1,40,8,128]{4,3,2,1,0:T(8,128)(2,1)} %legendre_synthesis.3), calls=%async_computation.2 | async-start | bytes 2621440 | tf_op jit(solution)/shard_map/all_to_all | solution.py:255
  14.9 19.0 %legendre_synthesis.2 = bf16[16,4,40,8,128]{4,3,2,1,0:T(8,128)(2,1)} custom-call(s32[40,2]{1,0:T(8,128)} %add_select_fusion.count_ref.refs_0_, bf16[40,2,2,32,320]{4,3,2,1,0:T(8,128)(2,1)} %spectral_ref.3, bf16[40,2,320,640]{3,2,1,0:T(8,128)(2,1)} %refs_2_.1), custom_call_target="tpu_custom_call" | custom-call | flops 419430400 | bytes 9830400 | tf_op jit(solution)/shard_map/legendre_synthesis/pallas_call | solution.py:86
  33.9 0.0 copy-start.3
  33.9 11.6 %all-to-all-done.2.y_ref = bf16[16,1,40,8,128]{4,3,2,1,0:T(8,128)(2,1)S(1)} async-done(((bf16[16,1,40,8,128]{4,3,2,1,0:T(8,128)(2,1)}), bf16[16,1,40,8,128]{4,3,2,1,0:T(8,128)(2,1)S(1)}, u32[]{:S(2)}, u32[]{:S(2)}) %all-to-all-start.2) | async-done | bytes 1310752 | tf_op jit(solution)/shard_map/all_to_all | solution.py:255
  45.4 0.0 copy-start.2
  45.4 1.1 copy-done.2
  46.5 4.9 %all-to-all-start = ((bf16[16,4,40,8,128]{4,3,2,1,0:T(8,128)(2,1)}), bf16[16,4,40,8,128]{4,3,2,1,0:T(8,128)(2,1)}, u32[]{:S(2)}, u32[]{:S(2)}) async-start(bf16[16,4,40,8,128]{4,3,2,1,0:T(8,128)(2,1)} %legendre_synthesis.2), calls=%async_computation | async-start | bytes 10485760 | tf_op jit(solution)/shard_map/all_to_all | solution.py:255
  51.4 0.0 copy-done.3
  51.4 0.9 reshape.8.alt_ref
  52.3 3.6 %multiply_subtract_fusion.1 = (f32[1296,640]{1,0:T(8,128)S(1)}, bf16[1296,640]{1,0:T(8,128)(2,1)}) fusion(f32[640]{0:T(1024)S(1)} %convert_element_type.19, f32[640]{0:T(1024)S(1)} %get-tuple-element.8), kind=kLoop, calls=%fused_computation.11 | loop fusion | flops 18247680 | bytes 4981760 | tf_op jit(solution)/shard_map/sub | solution.py:32
  55.9 4.0 %multiply_convert_fusion.2.ss_ref = bf16[1280,640]{1,0:T(8,128)(2,1)} fusion(f32[1296,640]{1,0:T(8,128)S(1)} %get-tuple-element.9, f32[640]{0:T(1024)S(1)} %get-tuple-element.8), kind=kLoop, calls=%fused_computation.37 | loop fusion | flops 17203200 | bytes 4917760 | tf_op jit(solution)/shard_map/convert_element_type | solution.py:51
  60.0 6.4 %fusion.13 = (bf16[640,1280]{1,0:T(8,128)(2,1)}, bf16[640,1280]{1,0:T(8,128)(2,1)}) fusion(f32[1280]{0:T(1024)S(1)} %get-tuple-element.12, f32[1280]{0:T(1024)S(1)} %get-tuple-element.11, f32[640]{0:T(1024)S(1)} %convert_element_type.19), kind=kLoop, calls=%fused_computation.22 | loop fusion | flops 34406400 | bytes 3289600 | tf_op jit(solution)/shard_map/convert_element_type | solution.py:56
  66.4 9.2 %grid_product.4 = bf16[16,1,40,8,128]{4,3,2,1,0:T(8,128)(2,1)} custom-call(bf16[16,1,40,8,128]{4,3,2,1,0:T(8,128)(2,1)} %copy-done.2, bf16[1296,640]{1,0:T(8,128)(2,1)} %get-tuple-element.10.sc_ref, bf16[1280,640]{1,0:T(8,128)(2,1)} %multiply_convert_fusion.2.ss_ref, bf16[640,1280]{1,0:T(8,128)(2,1)} %get-tuple-element.6.ac_ref, ...), custom_call_target="tpu_custom_call" | custom-call | flops 3355443200 | bytes 9175040 | tf_op jit(solution)/shard_map/grid_product/pallas_call | solution.py:147
  75.6 90.7 %all-to-all-done.y_ref = bf16[16,4,40,8,128]{4,3,2,1,0:T(8,128)(2,1)} async-done(((bf16[16,4,40,8,128]{4,3,2,1,0:T(8,128)(2,1)}), bf16[16,4,40,8,128]{4,3,2,1,0:T(8,128)(2,1)}, u32[]{:S(2)}, u32[]{:S(2)}) %all-to-all-start) | async-done | bytes 5242912 | tf_op jit(solution)/shard_map/all_to_all | solution.py:255
  166.3 4.9 %all-to-all-start.3 = ((bf16[16,1,40,8,128]{4,3,2,1,0:T(8,128)(2,1)}), bf16[16,1,40,8,128]{4,3,2,1,0:T(8,128)(2,1)S(1)}, u32[]{:S(2)}, u32[]{:S(2)}) async-start(bf16[16,1,40,8,128]{4,3,2,1,0:T(8,128)(2,1)} %grid_product.4), calls=%async_computation.3 | async-start | bytes 2621440 | tf_op jit(solution)/shard_map/all_to_all | solution.py:255
  171.3 18.9 %grid_product.5 = bf16[16,3,40,8,128]{4,3,2,1,0:T(8,128)(2,1)} custom-call(bf16[16,4,40,8,128]{4,3,2,1,0:T(8,128)(2,1)} %all-to-all-done.y_ref, bf16[1296,640]{1,0:T(8,128)(2,1)} %get-tuple-element.10.sc_ref, bf16[1280,640]{1,0:T(8,128)(2,1)} %multiply_convert_fusion.2.ss_ref, bf16[640,1280]{1,0:T(8,128)(2,1)} %get-tuple-element.6.ac_ref, ...), custom_call_target="tpu_custom_call" | custom-call | flops 10066329600 | bytes 14417920 | tf_op jit(solution)/shard_map/grid_product/pallas_call | solution.py:147
  190.1 11.7 %all-to-all-done.3.refs_1_ = bf16[16,1,40,8,128]{4,3,2,1,0:T(8,128)(2,1)S(1)} async-done(((bf16[16,1,40,8,128]{4,3,2,1,0:T(8,128)(2,1)}), bf16[16,1,40,8,128]{4,3,2,1,0:T(8,128)(2,1)S(1)}, u32[]{:S(2)}, u32[]{:S(2)}) %all-to-all-start.3) | async-done | bytes 1310752 | tf_op jit(solution)/shard_map/all_to_all | solution.py:255
  201.8 0.0 copy-start
  201.8 1.1 copy-done
  202.9 4.9 %all-to-all-start.4 = ((bf16[16,3,40,8,128]{4,3,2,1,0:T(8,128)(2,1)}), bf16[16,3,40,8,128]{4,3,2,1,0:T(8,128)(2,1)}, u32[]{:S(2)}, u32[]{:S(2)}) async-start(bf16[16,3,40,8,128]{4,3,2,1,0:T(8,128)(2,1)} %grid_product.5), calls=%async_computation.4 | async-start | bytes 7864320 | tf_op jit(solution)/shard_map/all_to_all | solution.py:255
  207.8 9.2 %grid_product.3 = bf16[16,1,40,8,128]{4,3,2,1,0:T(8,128)(2,1)} custom-call(bf16[16,4,40,8,128]{4,3,2,1,0:T(8,128)(2,1)} %all-to-all-done.y_ref, bf16[1296,640]{1,0:T(8,128)(2,1)} %get-tuple-element.10.sc_ref, bf16[1280,640]{1,0:T(8,128)(2,1)} %multiply_convert_fusion.2.ss_ref, bf16[640,1280]{1,0:T(8,128)(2,1)} %get-tuple-element.6.ac_ref, ...), custom_call_target="tpu_custom_call" | custom-call | flops 3355443200 | bytes 9175040 | tf_op jit(solution)/shard_map/grid_product/pallas_call | solution.py:147
  217.0 77.6 %all-to-all-done.4.refs_2_ = bf16[16,3,40,8,128]{4,3,2,1,0:T(8,128)(2,1)} async-done(((bf16[16,3,40,8,128]{4,3,2,1,0:T(8,128)(2,1)}), bf16[16,3,40,8,128]{4,3,2,1,0:T(8,128)(2,1)}, u32[]{:S(2)}, u32[]{:S(2)}) %all-to-all-start.4) | async-done | bytes 3932192 | tf_op jit(solution)/shard_map/all_to_all | solution.py:255
  294.6 4.9 %all-to-all-start.1 = ((bf16[16,1,40,8,128]{4,3,2,1,0:T(8,128)(2,1)}), bf16[16,1,40,8,128]{4,3,2,1,0:T(8,128)(2,1)S(1)}, u32[]{:S(2)}, u32[]{:S(2)}) async-start(bf16[16,1,40,8,128]{4,3,2,1,0:T(8,128)(2,1)} %grid_product.3), calls=%async_computation.1 | async-start | bytes 2621440 | tf_op jit(solution)/shard_map/all_to_all | solution.py:255
  299.5 17.8 %legendre_projection.2.refs_3_ = f32[40,2,2,32,320]{4,3,2,1,0:T(8,128)} custom-call(s32[40,2]{1,0:T(8,128)} %add_select_fusion.count_ref.refs_0_, bf16[16,1,40,8,128]{4,3,2,1,0:T(8,128)(2,1)} %copy-done, bf16[16,3,40,8,128]{4,3,2,1,0:T(8,128)(2,1)} %all-to-all-done.4.refs_2_, bf16[40,2,320,640]{3,2,1,0:T(8,128)(2,1)} %refs_2_.1, ...), custom_call_target="tpu_custom_call" | custom-call | flops 1677721600 | bytes 32768000 | tf_op jit(solution)/shard_map/legendre_projection/pallas_call | solution.py:222
  317.3 12.8 %all-to-all-done.1.refs_1_ = bf16[16,1,40,8,128]{4,3,2,1,0:T(8,128)(2,1)S(1)} async-done(((bf16[16,1,40,8,128]{4,3,2,1,0:T(8,128)(2,1)}), bf16[16,1,40,8,128]{4,3,2,1,0:T(8,128)(2,1)S(1)}, u32[]{:S(2)}, u32[]{:S(2)}) %all-to-all-start.1) | async-done | bytes 1310752 | tf_op jit(solution)/shard_map/all_to_all | solution.py:255
  330.1 0.0 copy-start.1
  330.1 1.1 copy-done.1
  331.2 9.8 %legendre_projection.3 = f32[40,2,2,32,320]{4,3,2,1,0:T(8,128)} custom-call(s32[40,2]{1,0:T(8,128)} %add_select_fusion.count_ref.refs_0_, bf16[16,1,40,8,128]{4,3,2,1,0:T(8,128)(2,1)} %copy-done.1, bf16[40,2,320,640]{3,2,1,0:T(8,128)(2,1)} %refs_2_.1, f32[40,2,2,32,320]{4,3,2,1,0:T(8,128)} %legendre_projection.2.refs_3_), custom_call_target="tpu_custom_call", output_to_operand_aliasing={{}: (3, {})} | custom-call | flops 419430400 | bytes 13107200 | tf_op jit(solution)/shard_map/legendre_projection/pallas_call | solution.py:222
  (3 shorter events, 0.0 us)
Async XLA Ops:
  8.3 37.1 %all-to-all-start.2 = ((bf16[16,1,40,8,128]{4,3,2,1,0:T(8,128)(2,1)}), bf16[16,1,40,8,128]{4,3,2,1,0:T(8,128)(2,1)S(1)}, u32[]{:S(2)}, u32[]{:S(2)}) async-start(bf16[16,1,40,8,128]{4,3,2,1,0:T(8,128)(2,1)} %legendre_synthesis.3), calls=%async_computation.2 | async-start | bytes 2621440 | tf_op jit(solution)/shard_map/all_to_all | solution.py:255
  33.9 17.5 %copy-start.3 = (s32[640]{0:T(1024)S(1)}, s32[640]{0:T(1024)}, u32[]{:S(2)}) copy-start(s32[640]{0:T(1024)} %param.5) | copy-start | bytes 7684
  45.4 1.1 copy-start.2
  46.5 119.8 %all-to-all-start = ((bf16[16,4,40,8,128]{4,3,2,1,0:T(8,128)(2,1)}), bf16[16,4,40,8,128]{4,3,2,1,0:T(8,128)(2,1)}, u32[]{:S(2)}, u32[]{:S(2)}) async-start(bf16[16,4,40,8,128]{4,3,2,1,0:T(8,128)(2,1)} %legendre_synthesis.2), calls=%async_computation | async-start | bytes 10485760 | tf_op jit(solution)/shard_map/all_to_all | solution.py:255
  166.3 35.5 %all-to-all-start.3 = ((bf16[16,1,40,8,128]{4,3,2,1,0:T(8,128)(2,1)}), bf16[16,1,40,8,128]{4,3,2,1,0:T(8,128)(2,1)S(1)}, u32[]{:S(2)}, u32[]{:S(2)}) async-start(bf16[16,1,40,8,128]{4,3,2,1,0:T(8,128)(2,1)} %grid_product.4), calls=%async_computation.3 | async-start | bytes 2621440 | tf_op jit(solution)/shard_map/all_to_all | solution.py:255
  201.8 1.1 copy-start
  202.9 91.7 %all-to-all-start.4 = ((bf16[16,3,40,8,128]{4,3,2,1,0:T(8,128)(2,1)}), bf16[16,3,40,8,128]{4,3,2,1,0:T(8,128)(2,1)}, u32[]{:S(2)}, u32[]{:S(2)}) async-start(bf16[16,3,40,8,128]{4,3,2,1,0:T(8,128)(2,1)} %grid_product.5), calls=%async_computation.4 | async-start | bytes 7864320 | tf_op jit(solution)/shard_map/all_to_all | solution.py:255
  294.6 35.5 %all-to-all-start.1 = ((bf16[16,1,40,8,128]{4,3,2,1,0:T(8,128)(2,1)}), bf16[16,1,40,8,128]{4,3,2,1,0:T(8,128)(2,1)S(1)}, u32[]{:S(2)}, u32[]{:S(2)}) async-start(bf16[16,1,40,8,128]{4,3,2,1,0:T(8,128)(2,1)} %grid_product.3), calls=%async_computation.1 | async-start | bytes 2621440 | tf_op jit(solution)/shard_map/all_to_all | solution.py:255
  330.1 1.1 copy-start.1
